TPU v7x, 128 devices: a whole 4x4x4 slice. The times are simulated.
128 devices in a mesh: pipe: 2 (over core), dp: 4 (over x), tensor: 16 (over z, y).
Axes of the slice: x: 4, y: 4, z: 4, core: 2. Of those that a mesh axis runs over, the one named last changes fastest.
Arguments:
- embedded: bfloat16 [512, 4096], P('dp', 'pipe'), may hold values from -6 to 6
- rotation_scaled: float32 [4096, 4096], P(('pipe', 'dp'), 'tensor'), as said below
- value_proj: bfloat16 [2, 4096, 1024], P('pipe', 'tensor'), may hold values from -0.09375 to 0.09375
- output_proj: bfloat16 [2, 1024, 4096], P('pipe', None, 'tensor'), may hold values from -0.1875 to 0.1875
- mid_exponent: int32 [2, 1024], P('pipe'), may hold values from -3 to -1
- cotangent: bfloat16 [512, 4096], P('dp', 'tensor'), may hold values from -6 to 6
Outputs:
- rotation_next: float32 [4096, 4096], P(('pipe', 'dp'), 'tensor')
Inputs may be any that keep to these rules, and one draw needn't show every extreme that they name: rotation_scaled / sqrt(4096) is orthogonal.
All inputs are finite; a program needn't handle non-finite values.
Results may differ from a plain program's by a relative error of at most 0.017.
Values may be sent and summed in bfloat16 or wider, within the bound.
A program may use at most 64 MiB of HBM per device.

v0:
```python
import math

import jax
import jax.numpy as jnp
from jax import lax
from jax.sharding import PartitionSpec as P

D = 4096
MB = 4
TOK_MB = 32


def from_behind(shard, axis, by):
    length = lax.axis_size(axis)
    pairs = [(i, i + by) for i in range(length) if 0 <= i + by < length]
    return lax.ppermute(shard, axis, pairs)


def spread(shard, axis, root):
    mine = lax.axis_index(axis) == root
    return lax.psum(jnp.where(mine, shard, jnp.zeros_like(shard)), axis)


def local(embedded, rotation_scaled, value_proj, output_proj, mid_exponent, cotangent):
    sections = lax.axis_size("pipe")
    section_index = lax.axis_index("pipe")
    column_count = cotangent.shape[1]
    group_rows = embedded.shape[0]
    branch_units = value_proj.shape[2]
    rotation = rotation_scaled / math.sqrt(D)
    rot_rows = lax.all_gather(rotation.astype(jnp.bfloat16), "dp", axis=0, tiled=True)
    embed_part = jnp.dot(embedded, rot_rows, preferred_element_type=jnp.float32)
    start_field = lax.psum(embed_part.astype(jnp.bfloat16), "pipe").astype(jnp.float32)
    start_blocks = start_field.astype(jnp.bfloat16).reshape(MB, TOK_MB, column_count)
    target_blocks = cotangent.reshape(MB, TOK_MB, column_count)
    weight_in = value_proj[0]
    weight_out = output_proj[0]
    bounds = jnp.exp2(mid_exponent[0].astype(jnp.float32))
    lowest = -8.0 * bounds
    highest = 7.0 * bounds
    tick_total = MB + sections - 1

    def forward_tick(tick_count, loop_state):
        received, stash_h, stash_y, stash_r = loop_state
        micro_batch = tick_count - section_index
        active = (micro_batch >= 0) & (micro_batch < MB)
        position = jnp.clip(micro_batch, 0, MB - 1)
        first_input = lax.dynamic_index_in_dim(start_blocks, position, 0, keepdims=False)
        hidden = jnp.where(section_index == 0, first_input, received)
        hidden_f = hidden.astype(jnp.float32)
        partial_value = jnp.dot(hidden, weight_in, preferred_element_type=jnp.float32)
        squares = jnp.sum(hidden_f * hidden_f, axis=1)
        summed, square_total = lax.psum((partial_value, squares), "tensor")
        inv_rms = lax.rsqrt(square_total / D + 1e-05)[:, None]
        clipped = jnp.clip(inv_rms * summed, lowest, highest).astype(jnp.bfloat16)
        branch_out = jnp.dot(clipped, weight_out, preferred_element_type=jnp.float32)
        result = (hidden_f + branch_out).astype(jnp.bfloat16)
        stash_h = jnp.where(
            active, lax.dynamic_update_index_in_dim(stash_h, hidden, position, 0), stash_h
        )
        stash_y = jnp.where(
            active, lax.dynamic_update_index_in_dim(stash_y, summed, position, 0), stash_y
        )
        stash_r = jnp.where(
            active, lax.dynamic_update_index_in_dim(stash_r, inv_rms, position, 0), stash_r
        )
        received = from_behind(result, "pipe", 1)
        return (received, stash_h, stash_y, stash_r)

    forward_state = (
        jnp.zeros((TOK_MB, column_count), jnp.bfloat16),
        jnp.zeros((MB, TOK_MB, column_count), jnp.bfloat16),
        jnp.zeros((MB, TOK_MB, branch_units), jnp.float32),
        jnp.ones((MB, TOK_MB, 1), jnp.float32),
    )
    forward_state = lax.fori_loop(0, tick_total, forward_tick, forward_state)
    saved_h, saved_y, saved_r = (forward_state[1], forward_state[2], forward_state[3])

    def backward_tick(tick_count, loop_state):
        received, stash_g = loop_state
        micro_batch = tick_count - (sections - 1 - section_index)
        active = (micro_batch >= 0) & (micro_batch < MB)
        position = jnp.clip(micro_batch, 0, MB - 1)
        target = lax.dynamic_index_in_dim(target_blocks, position, 0, keepdims=False)
        incoming = jnp.where(section_index == sections - 1, target, received)
        hidden = lax.dynamic_index_in_dim(saved_h, position, 0, keepdims=False)
        summed = lax.dynamic_index_in_dim(saved_y, position, 0, keepdims=False)
        inv_rms = lax.dynamic_index_in_dim(saved_r, position, 0, keepdims=False)
        back_part = lax.dot_general(
            incoming, weight_out, (((1,), (1,)), ((), ())), preferred_element_type=jnp.float32
        )
        back_total = lax.psum(back_part, "tensor")
        gated_rows = inv_rms * summed
        inside = (gated_rows >= lowest) & (gated_rows <= highest)
        scaled_grad = (inv_rms * jnp.where(inside, back_total, 0.0)).astype(jnp.bfloat16)
        linear = lax.dot_general(
            scaled_grad, weight_in, (((1,), (1,)), ((), ())), preferred_element_type=jnp.float32
        )
        statistic = jnp.sum(scaled_grad.astype(jnp.float32) * summed, axis=1, keepdims=True)
        grad_field = (
            incoming.astype(jnp.float32)
            + linear
            - inv_rms * inv_rms / D * statistic * hidden.astype(jnp.float32)
        )
        sent_grad = grad_field.astype(jnp.bfloat16)
        stash_g = jnp.where(
            active & (section_index == 0),
            lax.dynamic_update_index_in_dim(stash_g, sent_grad, position, 0),
            stash_g,
        )
        received = from_behind(sent_grad, "pipe", -1)
        return (received, stash_g)

    backward_state = (
        jnp.zeros((TOK_MB, column_count), jnp.bfloat16),
        jnp.zeros((MB, TOK_MB, column_count), jnp.bfloat16),
    )
    backward_state = lax.fori_loop(0, tick_total, backward_tick, backward_state)
    grad_local = backward_state[1].reshape(group_rows, column_count)
    grad_all = spread(grad_local, "pipe", 0)
    value_part = lax.dot_general(
        grad_all, rot_rows, (((1,), (1,)), ((), ())), preferred_element_type=jnp.float32
    )
    embed_grad = lax.psum(value_part.astype(jnp.bfloat16), "tensor")
    back_part = jnp.dot(embed_grad, rot_rows, preferred_element_type=jnp.float32)
    turned = lax.psum(back_part.astype(jnp.bfloat16), "pipe").astype(jnp.float32)
    first_dirs = (2.0 * jnp.concatenate([turned, -start_field], axis=0)).astype(jnp.bfloat16)
    left_rows = jnp.concatenate([embedded, embed_grad], axis=0)
    right_rows = jnp.concatenate([embed_grad, -embedded], axis=0)
    partial_value = left_rows
    step_one = lax.psum_scatter(
        lax.dot_general(
            partial_value, first_dirs, (((0,), (0,)), ((), ())), preferred_element_type=jnp.float32
        ),
        "dp",
        scatter_dimension=0,
        tiled=True,
    )
    norm_total = lax.psum(jnp.sum(step_one * step_one), ("pipe", "dp", "tensor"))
    step_rate = jnp.sqrt(D / (norm_total + 1e-06))
    first_iter = rotation - 0.5 * step_rate * step_one
    iterate = (rotation + first_iter).astype(jnp.bfloat16)
    iter_rows = lax.all_gather(iterate, "dp", axis=0, tiled=True)
    second_part = jnp.dot(right_rows, iter_rows, preferred_element_type=jnp.float32)
    second_dirs = lax.psum(second_part.astype(jnp.bfloat16), "pipe")
    partial_value = left_rows
    step_two = lax.psum_scatter(
        lax.dot_general(
            partial_value, second_dirs, (((0,), (0,)), ((), ())), preferred_element_type=jnp.float32
        ),
        "dp",
        scatter_dimension=0,
        tiled=True,
    )
    return math.sqrt(D) * (rotation - 0.5 * step_rate * step_two)


def solution(mesh):
    return jax.shard_map(
        local,
        mesh=mesh,
        in_specs=(
            P("dp", "pipe"),
            P(("pipe", "dp"), "tensor"),
            P("pipe", "tensor", None),
            P("pipe", None, "tensor"),
            P("pipe", None),
            P("dp", "tensor"),
        ),
        out_specs=P(("pipe", "dp"), "tensor"),
        check_vma=False,
    )
```

profile of v0, /device:TPU:1, one launch (start us, length us, event | category | flops | bytes accessed | tf_op | source)
XLA Modules:
  0.0 1303.0 jit_solution(10443372473404619989)
XLA Ops:
  8.5 25.7 %all-gather.3.cloned.1.call-done = bf16[2048,256]{1,0:T(8,128)(2,1)} async-done(((bf16[512,256]{1,0:T(8,128)(2,1)}), bf16[2048,256]{1,0:T(8,128)(2,1)}) %all-gather.3.cloned.1.call-update) | async-done | bytes 1048592 | tf_op jit(solution)/shard_map/all_gather | solution.py:31
  36.8 26.2 %all-reduce.8.cloned.1.call-done = bf16[128,256]{0,1:T(8,128)(2,1)} async-done(((bf16[128,256]{0,1:T(8,128)(2,1)}), bf16[128,256]{0,1:T(8,128)(2,1)}) %all-reduce.8.cloned.1.call-update) | async-done | bytes 65552 | tf_op jit(solution)/shard_map/psum | solution.py:33
  64.1 450.8 %while.37 = (s32[]{:T(128)}, bf16[32,256]{1,0:T(8,128)(2,1)S(1)}, bf16[4,32,256]{2,1,0:T(8,128)(2,1)S(1)}, f32[4,32,1024]{2,1,0:T(8,128)S(1)}, f32[4,32,1]{1,2,0...) while((s32[]{:T(128)}, bf16[32,256]{1,0:T(8,128)(2,1)S(1)}, ...), condition=%wide.region_5.6_spmd, body=%wide.region_1.5_spmd.sunk | while | flops 33882280 | bytes 2710062 | solution.py:76
  65.2 33.6 %psum.89 = f32[32]{0:T(128)S(1)} all-reduce(f32[32]{0:T(128)S(1)} %fusion.65), channel_id=1, replica_groups=mesh['pipe'=2,'dp'=4,'tensor'=16] {'tensor'}, use_global_device_ids=true, to_apply=%region_3.3 | all-reduce | flops 32 | bytes 256 | tf_op jit(solution)/shard_map/while/body/eval_jaxpr/psum | solution.py:53
  98.8 51.7 %all-reduce.18.cloned.1.call-done = f32[32,1024]{1,0:T(8,128)} async-done(((f32[32,1024]{1,0:T(8,128)}), f32[32,1024]{1,0:T(8,128)}) %all-reduce.18.cloned.1.call-update) | async-done | bytes 131088 | tf_op jit(solution)/shard_map/while/body/eval_jaxpr/psum | solution.py:53
  157.1 30.9 %psum.89 = f32[32]{0:T(128)S(1)} all-reduce(f32[32]{0:T(128)S(1)} %fusion.65), channel_id=1, replica_groups=mesh['pipe'=2,'dp'=4,'tensor'=16] {'tensor'}, use_global_device_ids=true, to_apply=%region_3.3 | all-reduce | flops 32 | bytes 256 | tf_op jit(solution)/shard_map/while/body/eval_jaxpr/psum | solution.py:53
  188.0 52.1 %all-reduce.18.cloned.1.call-done = f32[32,1024]{1,0:T(8,128)} async-done(((f32[32,1024]{1,0:T(8,128)}), f32[32,1024]{1,0:T(8,128)}) %all-reduce.18.cloned.1.call-update) | async-done | bytes 131088 | tf_op jit(solution)/shard_map/while/body/eval_jaxpr/psum | solution.py:53
  246.7 30.9 %psum.89 = f32[32]{0:T(128)S(1)} all-reduce(f32[32]{0:T(128)S(1)} %fusion.65), channel_id=1, replica_groups=mesh['pipe'=2,'dp'=4,'tensor'=16] {'tensor'}, use_global_device_ids=true, to_apply=%region_3.3 | all-reduce | flops 32 | bytes 256 | tf_op jit(solution)/shard_map/while/body/eval_jaxpr/psum | solution.py:53
  277.6 52.1 %all-reduce.18.cloned.1.call-done = f32[32,1024]{1,0:T(8,128)} async-done(((f32[32,1024]{1,0:T(8,128)}), f32[32,1024]{1,0:T(8,128)}) %all-reduce.18.cloned.1.call-update) | async-done | bytes 131088 | tf_op jit(solution)/shard_map/while/body/eval_jaxpr/psum | solution.py:53
  336.3 30.9 %psum.89 = f32[32]{0:T(128)S(1)} all-reduce(f32[32]{0:T(128)S(1)} %fusion.65), channel_id=1, replica_groups=mesh['pipe'=2,'dp'=4,'tensor'=16] {'tensor'}, use_global_device_ids=true, to_apply=%region_3.3 | all-reduce | flops 32 | bytes 256 | tf_op jit(solution)/shard_map/while/body/eval_jaxpr/psum | solution.py:53
  367.2 52.1 %all-reduce.18.cloned.1.call-done = f32[32,1024]{1,0:T(8,128)} async-done(((f32[32,1024]{1,0:T(8,128)}), f32[32,1024]{1,0:T(8,128)}) %all-reduce.18.cloned.1.call-update) | async-done | bytes 131088 | tf_op jit(solution)/shard_map/while/body/eval_jaxpr/psum | solution.py:53
  426.0 30.9 %psum.89 = f32[32]{0:T(128)S(1)} all-reduce(f32[32]{0:T(128)S(1)} %fusion.65), channel_id=1, replica_groups=mesh['pipe'=2,'dp'=4,'tensor'=16] {'tensor'}, use_global_device_ids=true, to_apply=%region_3.3 | all-reduce | flops 32 | bytes 256 | tf_op jit(solution)/shard_map/while/body/eval_jaxpr/psum | solution.py:53
  456.9 52.4 %all-reduce.18.cloned.1.call-done = f32[32,1024]{1,0:T(8,128)} async-done(((f32[32,1024]{1,0:T(8,128)}), f32[32,1024]{1,0:T(8,128)}) %all-reduce.18.cloned.1.call-update) | async-done | bytes 131088 | tf_op jit(solution)/shard_map/while/body/eval_jaxpr/psum | solution.py:53
  514.9 454.3 %while.38 = (s32[]{:T(128)}, bf16[32,256]{1,0:T(8,128)(2,1)S(1)}, bf16[4,32,256]{2,1,0:T(8,128)(2,1)S(1)}, pred[]{:T(512)}, s32[]{:T(128)}, /*index=5*/bf16[4,32...) while((s32[]{:T(128)}, bf16[32,256]{1,0:T(8,128)(2,1)S(1)}, ...), condition=%wide.region_9.10_spmd, body=%wide.region_6.9_spmd.sunk | while | flops 33988680 | bytes 2565832 | solution.py:118
  515.9 83.2 %all-reduce.20.cloned.1.call-done = f32[32,1024]{1,0:T(8,128)} async-done(((f32[32,1024]{1,0:T(8,128)}), f32[32,1024]{1,0:T(8,128)}) %all-reduce.20.cloned.1.call-update) | async-done | bytes 131088 | tf_op jit(solution)/shard_map/while/body/eval_jaxpr/psum | solution.py:92
  606.8 83.3 %all-reduce.20.cloned.1.call-done = f32[32,1024]{1,0:T(8,128)} async-done(((f32[32,1024]{1,0:T(8,128)}), f32[32,1024]{1,0:T(8,128)}) %all-reduce.20.cloned.1.call-update) | async-done | bytes 131088 | tf_op jit(solution)/shard_map/while/body/eval_jaxpr/psum | solution.py:92
  697.8 83.0 %all-reduce.20.cloned.1.call-done = f32[32,1024]{1,0:T(8,128)} async-done(((f32[32,1024]{1,0:T(8,128)}), f32[32,1024]{1,0:T(8,128)}) %all-reduce.20.cloned.1.call-update) | async-done | bytes 131088 | tf_op jit(solution)/shard_map/while/body/eval_jaxpr/psum | solution.py:92
  788.5 83.3 %all-reduce.20.cloned.1.call-done = f32[32,1024]{1,0:T(8,128)} async-done(((f32[32,1024]{1,0:T(8,128)}), f32[32,1024]{1,0:T(8,128)}) %all-reduce.20.cloned.1.call-update) | async-done | bytes 131088 | tf_op jit(solution)/shard_map/while/body/eval_jaxpr/psum | solution.py:92
  879.4 83.0 %all-reduce.20.cloned.1.call-done = f32[32,1024]{1,0:T(8,128)} async-done(((f32[32,1024]{1,0:T(8,128)}), f32[32,1024]{1,0:T(8,128)}) %all-reduce.20.cloned.1.call-update) | async-done | bytes 131088 | tf_op jit(solution)/shard_map/while/body/eval_jaxpr/psum | solution.py:92
  997.4 85.5 %all-reduce.12.cloned.1.call-done = bf16[128,2048]{1,0:T(8,128)(2,1)} async-done(((bf16[128,2048]{1,0:T(8,128)(2,1)}), bf16[128,2048]{1,0:T(8,128)(2,1)}) %all-reduce.12.cloned.1.call-update) | async-done | bytes 524304 | tf_op jit(solution)/shard_map/psum | solution.py:124
  1113.0 30.7 %reduce-scatter.3.cloned.1.call-done = f32[512,256]{1,0:T(8,128)} async-done(((f32[2048,256]{1,0:T(8,128)}), f32[512,256]{1,0:T(8,128)}) %reduce-scatter.3.cloned.1.call-update) | async-done | bytes 524304 | tf_op jit(solution)/shard_map/reduce_scatter | solution.py:131
  1145.4 64.8 %psum.83 = f32[]{:T(128)} all-reduce(f32[]{:T(128)} %multiply_reduce_fusion), channel_id=1, replica_groups=mesh['pipe'=2,'dp'=4,'tensor'=16] {'pipe','dp','tensor'}, use_global_device_ids=true, to_apply=%region_15.16 | all-reduce | flops 1 | bytes 8 | tf_op jit(solution)/shard_map/psum | solution.py:139
  1234.7 26.5 %all-reduce.16.cloned.1.call-done = bf16[256,256]{1,0:T(8,128)(2,1)} async-done(((bf16[256,256]{1,0:T(8,128)(2,1)}), bf16[256,256]{1,0:T(8,128)(2,1)}) %all-reduce.16.cloned.1.call-update) | async-done | bytes 131088 | tf_op jit(solution)/shard_map/psum | solution.py:145
  1263.9 30.7 %reduce-scatter.5.cloned.1.call-done = f32[512,256]{1,0:T(8,128)} async-done(((f32[2048,256]{1,0:T(8,128)}), f32[512,256]{1,0:T(8,128)}) %reduce-scatter.5.cloned.1.call-update) | async-done | bytes 524304 | tf_op jit(solution)/shard_map/reduce_scatter | solution.py:147
  (164 shorter events, 165.1 us)
Async XLA Ops:
  6.5 27.7 %all-gather.3.cloned.1.call-start = ((), (), s32[]{:S(2)}) async-start(), calls=%async_computation.2 | async-start | bytes 1310720 | tf_op jit(solution)/shard_map/all_gather | solution.py:31
  8.4 54.6 %all-reduce.8.cloned.1.call-start = ((), (), s32[]{:S(2)}) async-start(), calls=%async_computation.3 | async-start | bytes 131072 | tf_op jit(solution)/shard_map/psum | solution.py:33
  64.1 86.3 %all-reduce.18.cloned.1.call-start = ((), (), s32[]{:S(2)}) async-start(), calls=%async_computation.11 | async-start | bytes 262144 | tf_op jit(solution)/shard_map/while/body/eval_jaxpr/psum | solution.py:53
  156.1 84.0 %all-reduce.18.cloned.1.call-start = ((), (), s32[]{:S(2)}) async-start(), calls=%async_computation.11 | async-start | bytes 262144 | tf_op jit(solution)/shard_map/while/body/eval_jaxpr/psum | solution.py:53
  245.7 84.0 %all-reduce.18.cloned.1.call-start = ((), (), s32[]{:S(2)}) async-start(), calls=%async_computation.11 | async-start | bytes 262144 | tf_op jit(solution)/shard_map/while/body/eval_jaxpr/psum | solution.py:53
  335.3 84.0 %all-reduce.18.cloned.1.call-start = ((), (), s32[]{:S(2)}) async-start(), calls=%async_computation.11 | async-start | bytes 262144 | tf_op jit(solution)/shard_map/while/body/eval_jaxpr/psum | solution.py:53
  424.9 84.3 %all-reduce.18.cloned.1.call-start = ((), (), s32[]{:S(2)}) async-start(), calls=%async_computation.11 | async-start | bytes 262144 | tf_op jit(solution)/shard_map/while/body/eval_jaxpr/psum | solution.py:53
  514.9 84.3 %all-reduce.20.cloned.1.call-start = ((), (), s32[]{:S(2)}) async-start(), calls=%async_computation.12 | async-start | bytes 262144 | tf_op jit(solution)/shard_map/while/body/eval_jaxpr/psum | solution.py:92
  600.6 5.3 collective-permute-start.1
  605.9 84.3 %all-reduce.20.cloned.1.call-start = ((), (), s32[]{:S(2)}) async-start(), calls=%async_computation.12 | async-start | bytes 262144 | tf_op jit(solution)/shard_map/while/body/eval_jaxpr/psum | solution.py:92
  691.6 5.3 collective-permute-start.1
  696.8 84.0 %all-reduce.20.cloned.1.call-start = ((), (), s32[]{:S(2)}) async-start(), calls=%async_computation.12 | async-start | bytes 262144 | tf_op jit(solution)/shard_map/while/body/eval_jaxpr/psum | solution.py:92
  782.2 5.3 collective-permute-start.1
  787.5 84.3 %all-reduce.20.cloned.1.call-start = ((), (), s32[]{:S(2)}) async-start(), calls=%async_computation.12 | async-start | bytes 262144 | tf_op jit(solution)/shard_map/while/body/eval_jaxpr/psum | solution.py:92
  873.2 5.3 collective-permute-start.1
  878.5 84.0 %all-reduce.20.cloned.1.call-start = ((), (), s32[]{:S(2)}) async-start(), calls=%async_computation.12 | async-start | bytes 262144 | tf_op jit(solution)/shard_map/while/body/eval_jaxpr/psum | solution.py:92
  963.9 5.3 collective-permute-start.1
  969.1 25.9 %all-reduce.10.cloned.1.call-start = ((), (), s32[]{:S(2)}) async-start(), calls=%async_computation.4 | async-start | bytes 131072 | tf_op jit(solution)/shard_map/psum | solution.py:21
  969.9 113.0 %all-reduce.12.cloned.1.call-start = ((), (), s32[]{:S(2)}) async-start(), calls=%async_computation.5 | async-start | bytes 1048576 | tf_op jit(solution)/shard_map/psum | solution.py:124
  997.2 113.1 %all-reduce.14.cloned.1.call-start = ((), (), s32[]{:S(2)}) async-start(), calls=%async_computation.6 | async-start | bytes 131072 | tf_op jit(solution)/shard_map/psum | solution.py:126
  1085.1 58.6 %reduce-scatter.3.cloned.1.call-start = ((), (), s32[]{:S(2)}) async-start(), calls=%async_computation.7 | async-start | bytes 2621440 | tf_op jit(solution)/shard_map/reduce_scatter | solution.py:131
  1112.9 119.3 %all-gather.5.cloned.1.call-start = ((), (), s32[]{:S(2)}) async-start(), calls=%async_computation.8 | async-start | bytes 1310720 | tf_op jit(solution)/shard_map/all_gather | solution.py:143
  1212.9 48.3 %all-reduce.16.cloned.1.call-start = ((), (), s32[]{:S(2)}) async-start(), calls=%async_computation.9 | async-start | bytes 262144 | tf_op jit(solution)/shard_map/psum | solution.py:145
  1234.6 60.0 %reduce-scatter.5.cloned.1.call-start = ((), (), s32[]{:S(2)}) async-start(), calls=%async_computation.10 | async-start | bytes 2621440 | tf_op jit(solution)/shard_map/reduce_scatter | solution.py:147
  (14 other events, 1372.3 us)
Sparse Core Ops, SparseCore 0:
  9.0 25.1 all-gather.2
  36.8 26.1 all-reduce.7
  68.1 82.2 all-reduce.17
  159.8 80.2 all-reduce.17
  249.4 80.2 all-reduce.17
  339.0 80.2 all-reduce.17
  428.9 80.2 all-reduce.17
  518.9 80.2 all-reduce.19
  609.8 80.2 all-reduce.19
  700.5 80.2 all-reduce.19
  791.5 80.2 all-reduce.19
  882.1 80.2 all-reduce.19
  972.3 22.6 all-reduce.9
  998.1 84.6 all-reduce.11
  1085.2 25.0 all-reduce.13
  1113.1 30.5 reduce-scatter.2
  1213.0 19.2 all-gather.4
  1234.8 26.3 all-reduce.15
  1264.0 30.5 reduce-scatter.4
where the time goes:
time: 1300 us
  waiting for transfers between devices  986 us (76%)
  blocking collectives  222 us (17%)
  matrix products  29.6 us (2%)
  starting transfers between devices  29.1 us (2%)
  other arithmetic  20 us (2%)
  between operations  14.1 us (1%)
    psum x5, waiting for transfers between devices, backward_tick(): back_total = lax.psum(back_part, 'tensor')  416 us
    psum x5, waiting for transfers between devices, forward_tick(): summed, square_total = lax.psum((partial_value, squares), 'tensor')  260 us
    psum x5, blocking collectives, forward_tick(): summed, square_total = lax.psum((partial_value, squares), 'tensor')  157 us
    psum x1, waiting for transfers between devices, local(): embed_grad = lax.psum(value_part.astype(jnp.bfloat16), 'tensor')  85.5 us
    psum x1, blocking collectives, local(): lax.psum(jnp.sum(step_one * step_one), ('pipe', 'dp', 'tensor'))  64.8 us
    reduce_scatter x1, waiting for transfers between devices, local(): lax.psum_scatter(lax.dot_general(partial_value, second_dirs, (((0,), (0,)...  30.7 us
    reduce_scatter x1, waiting for transfers between devices, local(): lax.psum_scatter(lax.dot_general(partial_value, first_dirs, (((0,), (0,))...  30.7 us
    ppermute x10, starting transfers between devices, from_behind(): return lax.ppermute(shard, axis, pairs)  28.6 us
  transfers between devices with their start and end apart: 29, of which 29 were waited for; matrix products, arithmetic and copies ran while one was open for 1% of the time, Pallas kernels for 0%

commit v1 on v0

v1 whole, which is shorter than its diff:
```python
import functools
import math

import jax
import jax.numpy as jnp
from jax import lax
from jax.experimental import pallas as pl
from jax.experimental.pallas import tpu as pltpu
from jax.sharding import PartitionSpec as P

BF = jnp.bfloat16
F32 = jnp.float32
LANES = 128
NT_DIMS = (((1,), (1,)), ((), ()))


def dot(a, b):
    return jnp.dot(a, b, preferred_element_type=F32)


def dot_nt(a, b):
    return lax.dot_general(a, b, NT_DIMS, preferred_element_type=F32)


def kernel(
    nd,
    nt,
    width,
    e_ref,
    r_ref,
    v_ref,
    o_ref,
    m_ref,
    u_ref,
    out_ref,
    rg,
    xpart,
    xrecv,
    xall,
    eall,
    gall,
    v1,
    bnd,
    bnd1,
    dcbuf,
    dc1recv,
    ybuf,
    y0recv,
    y1recv,
    cbuf,
    qbuf,
    dc0recv,
    q0buf,
    vpart,
    vrecv,
    vall,
    msbuf,
    msrecv,
    msall,
    nsbuf,
    nsrecv,
    nstbuf,
    nstrecv,
    tsend,
    trecv,
    xsend,
    xrecv_sem,
    gsend,
    grecv,
    psend,
    precv,
):
    p = lax.axis_index("pipe")
    d = lax.axis_index("dp")
    t = lax.axis_index("tensor")
    tg = u_ref.shape[0]
    half = ybuf.shape[2] - LANES
    own = tg // (nt // 2)
    rows = rg.shape[1]
    group = 2 * nd
    slot = p * nd + d
    my_half = lax.rem(t, 2)
    my_tok = pl.multiple_of((t // 2) * own, own)

    def rcopy(src, dst, ssem, rsem, to):
        return pltpu.make_async_remote_copy(
            src_ref=src,
            dst_ref=dst,
            send_sem=ssem,
            recv_sem=rsem,
            device_id=to,
            device_id_type=pl.DeviceIdType.MESH,
        )

    def loop(n, body):
        def step(k, carry):
            body(k)
            return carry

        lax.fori_loop(1, n, step, 0)

    def plane(k):
        return lax.rem(t + k, nt)

    def plane_back(k):
        return lax.rem(t + nt - k, nt)

    def piece(buf, j):
        return buf.at[lax.rem(j, 2), pl.ds(pl.multiple_of((j // 2) * own, own), own)]

    def rs_copy(buf, recv, ph, k):
        j = plane(k)
        return rcopy(piece(buf, j), recv.at[k], tsend.at[ph, k], trecv.at[ph, k], (p, d, j))

    def rs_start(buf, recv, ph):
        loop(nt, lambda k: rs_copy(buf, recv, ph, k).start())

    def rs_wait(buf, recv, ph):
        loop(nt, lambda k: rs_copy(buf, recv, ph, k).wait_recv())
        total = buf[my_half, pl.ds(my_tok, own)].astype(F32)
        for k in range(1, nt):
            total = total + recv[k].astype(F32)
        return total

    def ag_copy(buf, ph, k, j):
        return rcopy(piece(buf, j), piece(buf, j), tsend.at[ph, k], trecv.at[ph, k], (p, d, plane(k)))

    def ag_start(buf, ph):
        loop(nt, lambda k: ag_copy(buf, ph, k, t).start())

    def ag_wait(buf, ph):
        loop(nt, lambda k: ag_copy(buf, ph, k, plane_back(k)).wait_recv())

    def ring(k):
        return lax.rem(d + k, nd)

    def ring_back(k):
        return lax.rem(d + nd - k, nd)

    partner = (1 - p, d, t)

    bar = pltpu.get_barrier_semaphore()

    def greet(to):
        pl.semaphore_signal(bar, inc=1, device_id=to, device_id_type=pl.DeviceIdType.MESH)

    loop(nt, lambda k: greet((p, d, plane(k))))
    loop(nd, lambda k: greet((p, ring(k), t)))
    loop(nd, lambda k: greet((1 - p, ring(k), t)))
    greet(partner)

    rg[pl.ds(d, 1)] = (r_ref[...] * (1.0 / math.sqrt(width))).astype(BF)[None]
    bnd[...] = jnp.broadcast_to(jnp.exp2(m_ref[...].astype(F32)), bnd.shape)

    pl.semaphore_wait(bar, nt - 1 + 2 * (nd - 1) + 1)

    def r_copy(k, s):
        return rcopy(rg.at[s], rg.at[s], xsend.at[0, k], xrecv_sem.at[0, k], (p, ring(k), t))

    loop(nd, lambda k: r_copy(k, d).start())

    v1_copy = rcopy(v_ref.at[0], v1, psend.at[0], precv.at[0], partner)
    b1_copy = rcopy(bnd, bnd1, psend.at[1], precv.at[1], partner)
    d1_copy = rcopy(dcbuf, dcbuf, psend.at[2], precv.at[2], partner)

    @pl.when(p == 1)
    def _():
        part = dot_nt(u_ref[...], o_ref[0])
        dcbuf[0] = part[:, :half].astype(BF)
        dcbuf[1] = part[:, half:].astype(BF)
        d1_copy.start()
        b1_copy.start()
        v1_copy.start()

    @pl.when(p == 0)
    def _():
        d1_copy.wait_recv()
        rs_start(dcbuf, dc1recv, 0)

    loop(nd, lambda k: r_copy(k, ring_back(k)).wait_recv())
    part = dot(e_ref[...], rg[...].reshape(nd * rows, rg.shape[2])).astype(BF)
    xpart[...] = part
    x_copy = rcopy(xpart, xrecv, psend.at[3], precv.at[3], partner)
    x_copy.start()
    x_copy.wait_recv()
    hid0 = (xpart[...].astype(F32) + xrecv[...].astype(F32)).astype(BF)
    xall[pl.ds(d, 1)] = hid0[None]

    def h_copy(k, s):
        return rcopy(xall.at[s], xall.at[s], xsend.at[1, k], xrecv_sem.at[1, k], (p, ring(k), t))

    def e_copy(k, src, dst):
        cols = pl.ds(pl.multiple_of(src * rows, LANES), rows)
        return rcopy(e_ref.at[:, cols], eall.at[dst], xsend.at[2, k], xrecv_sem.at[2, k], (p, ring(k), t))

    def g_copy(k, to, s):
        return rcopy(gall.at[s], gall.at[s], gsend.at[k], grecv.at[k], to)

    @pl.when(p == 0)
    def _():
        def store_y(y, h):
            hf = h.astype(F32)
            sq = jnp.broadcast_to(jnp.sum(hf * hf, axis=1, keepdims=True), (tg, LANES))
            ybuf[0, :, :half] = y[:, :half]
            ybuf[1, :, :half] = y[:, half:]
            ybuf[0, :, half:] = sq
            ybuf[1, :, half:] = sq

        def pick(b):
            return jnp.where(my_half == 0, b[0:1, :half], b[0:1, half:])

        def norm(total):
            return lax.rsqrt(total[:, half : half + 1] / width + 1e-05)

        def store_q(buf, q, coef):
            hi = coef.astype(BF)
            lo = (coef - hi.astype(F32)).astype(BF)
            lane = lax.broadcasted_iota(jnp.int32, (own, LANES), 1)
            ext = jnp.where(
                lane < LANES // 2,
                jnp.broadcast_to(hi.astype(F32), (own, LANES)),
                jnp.broadcast_to(lo.astype(F32), (own, LANES)),
            )
            buf[my_half, pl.ds(my_tok, own), pl.ds(0, half)] = q
            buf[my_half, pl.ds(my_tok, own), pl.ds(half, LANES)] = ext.astype(BF)

        def load_coef(buf):
            ext = buf[0, :, half:].astype(F32) + buf[1, :, half:].astype(F32)
            return jnp.sum(ext, axis=1, keepdims=True) * (2.0 / LANES)

        def gate(total, dc, inv, bound, buf):
            y = total[:, :half]
            z = inv * y
            inside = (z >= -8.0 * bound) & (z <= 7.0 * bound)
            q = (inv * jnp.where(inside, dc, 0.0)).astype(BF)
            stat = jnp.sum(q.astype(F32) * y, axis=1, keepdims=True)
            store_q(buf, q, inv * inv / width * stat)

        h0 = xall[d]
        store_y(dot(h0, v_ref[0]), h0)
        rs_start(ybuf, y0recv, 1)
        loop(nd, lambda k: h_copy(k, d).start())
        loop(nd, lambda k: e_copy(k, ring(k), d).start())
        eall[pl.ds(d, 1)] = e_ref[:, pl.ds(pl.multiple_of(d * rows, LANES), rows)][None]
        tot0 = rs_wait(ybuf, y0recv, 1)
        inv0 = norm(tot0)
        bound0 = pick(bnd)
        c0 = jnp.clip(inv0 * tot0[:, :half], -8.0 * bound0, 7.0 * bound0).astype(BF)
        cbuf[my_half, pl.ds(my_tok, own)] = c0
        ag_start(cbuf, 2)
        loop(nt, lambda k: rs_copy(ybuf, y0recv, 1, k).wait_send())
        ag_wait(cbuf, 2)
        wo = o_ref[0]
        branch = dot(cbuf[0], wo[:half]) + dot(cbuf[1], wo[half:])
        h1 = (xall[d].astype(F32) + branch).astype(BF)
        v1_copy.wait_recv()
        b1_copy.wait_recv()
        store_y(dot(h1, v1[...]), h1)
        rs_start(ybuf, y1recv, 3)
        loop(nt, lambda k: rs_copy(dcbuf, dc1recv, 0, k).wait_send())
        dc1 = rs_wait(dcbuf, dc1recv, 0)
        tot1 = rs_wait(ybuf, y1recv, 3)
        gate(tot1, dc1, norm(tot1), pick(bnd1), qbuf)
        ag_start(qbuf, 4)
        ag_wait(qbuf, 4)
        w1 = v1[...]
        lin1 = dot_nt(qbuf[0, :, :half], w1[:, :half]) + dot_nt(qbuf[1, :, :half], w1[:, half:])
        u1 = (u_ref[...].astype(F32) + lin1 - load_coef(qbuf) * h1.astype(F32)).astype(BF)
        dpart = dot_nt(u1, o_ref[0])
        dcbuf[0] = dpart[:, :half].astype(BF)
        dcbuf[1] = dpart[:, half:].astype(BF)
        rs_start(dcbuf, dc0recv, 5)
        dc0 = rs_wait(dcbuf, dc0recv, 5)
        gate(tot0, dc0, inv0, bound0, q0buf)
        ag_start(q0buf, 6)
        ag_wait(q0buf, 6)
        w0 = v_ref[0]
        lin0 = dot_nt(q0buf[0, :, :half], w0[:, :half]) + dot_nt(q0buf[1, :, :half], w0[:, half:])
        g0 = (u1.astype(F32) + lin0 - load_coef(q0buf) * xall[d].astype(F32)).astype(BF)
        gall[pl.ds(d, 1)] = g0[None]
        loop(nd, lambda k: g_copy(k, (0, ring(k), t), d).start())
        g_copy(0, partner, d).start()
        loop(nd, lambda k: g_copy(nd + k, (1, ring(k), t), d).start())
        loop(nd, lambda k: g_copy(k, (0, ring(k), t), ring_back(k)).wait_recv())
        loop(nt, lambda k: ag_copy(cbuf, 2, k, t).wait_send())
        loop(nt, lambda k: rs_copy(ybuf, y1recv, 3, k).wait_send())
        loop(nt, lambda k: ag_copy(qbuf, 4, k, t).wait_send())
        loop(nt, lambda k: rs_copy(dcbuf, dc0recv, 5, k).wait_send())
        loop(nt, lambda k: ag_copy(q0buf, 6, k, t).wait_send())
        loop(nd, lambda k: g_copy(k, (0, ring(k), t), d).wait_send())
        g_copy(0, partner, d).wait_send()
        loop(nd, lambda k: g_copy(nd + k, (1, ring(k), t), d).wait_send())

    @pl.when(p == 1)
    def _():
        loop(nd, lambda k: h_copy(k, d).start())
        loop(nd, lambda k: e_copy(k, ring(k), d).start())
        eall[pl.ds(d, 1)] = e_ref[:, pl.ds(pl.multiple_of(d * rows, LANES), rows)][None]
        d1_copy.wait_send()
        b1_copy.wait_send()
        v1_copy.wait_send()
        g_copy(0, partner, d).wait_recv()
        loop(nd, lambda k: g_copy(nd + k, (1, ring(k), t), ring_back(k)).wait_recv())

    tokens = nd * tg
    grad = gall[...].reshape(tokens, gall.shape[2])
    vpart[...] = dot_nt(rg[d], grad).astype(BF)
    vrow = rows // nt

    def vpiece(buf, j):
        return buf.at[pl.ds(pl.multiple_of(j * vrow, vrow), vrow)]

    def vrs(k):
        j = plane(k)
        return rcopy(vpiece(vpart, j), vrecv.at[k], tsend.at[7, k], trecv.at[7, k], (p, d, j))

    def vag(k, j):
        return rcopy(vpiece(vall, j), vpiece(vall, j), tsend.at[8, k], trecv.at[8, k], (p, d, plane(k)))

    loop(nt, lambda k: vrs(k).start())
    loop(nd, lambda k: h_copy(k, ring_back(k)).wait_recv())
    loop(nd, lambda k: e_copy(k, d, ring_back(k)).wait_recv())
    emb = eall[...].reshape(tokens, rows)
    emb_t = emb.T
    front = dot(emb_t, grad)
    loop(nt, lambda k: vrs(k).wait_recv())
    vsum = vpart[pl.ds(pl.multiple_of(t * vrow, vrow), vrow)].astype(F32)
    for k in range(1, nt):
        vsum = vsum + vrecv[k].astype(F32)
    vall[pl.ds(pl.multiple_of(t * vrow, vrow), vrow)] = vsum.astype(BF)
    loop(nt, lambda k: vag(k, t).start())
    loop(nt, lambda k: vag(k, plane_back(k)).wait_recv())
    vt = vall[...]
    hid = xall[...].reshape(tokens, xall.shape[2])
    s0 = 2.0 * (front - dot(vt, hid))
    nsbuf[...] = jnp.broadcast_to(jnp.sum(s0 * s0), nsbuf.shape)
    s0b = s0.astype(BF)
    msbuf[pl.ds(0, nd)] = dot(vt.T, s0b).astype(BF).reshape(nd, tg, -1)
    msbuf[pl.ds(nd, nd)] = (-dot(emb, s0b)).astype(BF).reshape(nd, tg, -1)

    def cell(j):
        return (j // nd, lax.rem(j, nd), t)

    def fwd(k):
        return lax.rem(slot + k, group)

    def back(k):
        return lax.rem(slot + group - k, group)

    def ns_copy(k):
        return rcopy(nsbuf, nsrecv.at[k], gsend.at[group + k], grecv.at[group + k], cell(fwd(k)))

    def ms_copy(k):
        return rcopy(msbuf.at[fwd(k)], msrecv.at[k], gsend.at[2 * group + k], grecv.at[2 * group + k], cell(fwd(k)))

    def ma_copy(k, j):
        return rcopy(msall.at[j], msall.at[j], gsend.at[3 * group + k], grecv.at[3 * group + k], cell(fwd(k)))

    def nst_copy(k):
        return rcopy(nstbuf, nstrecv.at[k], tsend.at[9, k], trecv.at[9, k], (p, d, plane(k)))

    loop(group, lambda k: ns_copy(k).start())
    loop(group, lambda k: ms_copy(k).start())
    loop(group, lambda k: ns_copy(k).wait_recv())
    ns = nsbuf[...]
    for k in range(1, group):
        ns = ns + nsrecv[k]
    nstbuf[...] = ns
    loop(nt, lambda k: nst_copy(k).start())
    loop(group, lambda k: ms_copy(k).wait_recv())
    ms = msbuf[slot].astype(F32)
    for k in range(1, group):
        ms = ms + msrecv[k].astype(F32)
    msall[pl.ds(slot, 1)] = ms.astype(BF)[None]
    loop(group, lambda k: ma_copy(k, slot).start())
    loop(nt, lambda k: nst_copy(k).wait_recv())
    for k in range(1, nt):
        ns = ns + nstrecv[k]
    rate = jnp.sqrt(width / (ns[0:1, 0:1] + 1e-06))
    loop(group, lambda k: ma_copy(k, back(k)).wait_recv())
    mall = msall[...].astype(F32).reshape(2 * tokens, -1)
    first = (2.0 * grad.astype(F32) - 0.5 * rate * mall[:tokens]).astype(BF)
    second = (-2.0 * hid.astype(F32) - 0.5 * rate * mall[tokens:]).astype(BF)
    s1 = dot(emb_t, first) + dot(vt, second)
    out_ref[...] = r_ref[...] - (0.5 * math.sqrt(width)) * rate * s1

    loop(nd, lambda k: r_copy(k, d).wait_send())
    x_copy.wait_send()
    loop(nd, lambda k: h_copy(k, d).wait_send())
    loop(nd, lambda k: e_copy(k, ring(k), d).wait_send())
    loop(nt, lambda k: vrs(k).wait_send())
    loop(nt, lambda k: vag(k, t).wait_send())
    loop(group, lambda k: ns_copy(k).wait_send())
    loop(group, lambda k: ms_copy(k).wait_send())
    loop(group, lambda k: ma_copy(k, slot).wait_send())
    loop(nt, lambda k: nst_copy(k).wait_send())


def solution(mesh):
    nd = mesh.shape["dp"]
    nt = mesh.shape["tensor"]

    def local(embedded, rotation, value_proj, output_proj, mid_exponent, cotangent):
        tg = embedded.shape[0]
        rows, cols = rotation.shape
        width = cols * nt
        units = value_proj.shape[2]
        half = units // 2
        own = tg // (nt // 2)
        group = 2 * nd
        vm = pltpu.VMEM
        dma = pltpu.SemaphoreType.DMA
        scratch = [
            vm((nd, rows, cols), BF),
            vm((tg, cols), BF),
            vm((tg, cols), BF),
            vm((nd, tg, cols), BF),
            vm((nd, tg, rows), BF),
            vm((nd, tg, cols), BF),
            vm((cols, units), BF),
            vm((8, units), F32),
            vm((8, units), F32),
            vm((2, tg, half), BF),
            vm((nt, own, half), BF),
            vm((2, tg, half + LANES), F32),
            vm((nt, own, half + LANES), F32),
            vm((nt, own, half + LANES), F32),
            vm((2, tg, half), BF),
            vm((2, tg, half + LANES), BF),
            vm((nt, own, half), BF),
            vm((2, tg, half + LANES), BF),
            vm((rows, nd * tg), BF),
            vm((nt, rows // nt, nd * tg), BF),
            vm((rows, nd * tg), BF),
            vm((group, tg, cols), BF),
            vm((group, tg, cols), BF),
            vm((group, tg, cols), BF),
            vm((8, LANES), F32),
            vm((group, 8, LANES), F32),
            vm((8, LANES), F32),
            vm((nt, 8, LANES), F32),
            dma((10, nt)),
            dma((10, nt)),
            dma((3, nd)),
            dma((3, nd)),
            dma((4 * group,)),
            dma((4 * group,)),
            dma((4,)),
            dma((4,)),
        ]
        return pl.pallas_call(
            functools.partial(kernel, nd, nt, float(width)),
            out_shape=jax.ShapeDtypeStruct((rows, cols), F32),
            in_specs=[pl.BlockSpec(memory_space=pltpu.VMEM)] * 6,
            out_specs=pl.BlockSpec(memory_space=pltpu.VMEM),
            scratch_shapes=scratch,
            compiler_params=pltpu.CompilerParams(
                collective_id=0, has_side_effects=True, vmem_limit_bytes=48 << 20
            ),
        )(embedded, rotation, value_proj, output_proj, mid_exponent, cotangent)

    return jax.shard_map(
        local,
        mesh=mesh,
        in_specs=(
            P("dp", "pipe"),
            P(("pipe", "dp"), "tensor"),
            P("pipe", "tensor", None),
            P("pipe", None, "tensor"),
            P("pipe", None),
            P("dp", "tensor"),
        ),
        out_specs=P(("pipe", "dp"), "tensor"),
        check_vma=False,
    )
```

time: 1300 us -> 114 us (0.09)
  waiting for transfers between devices: 986 us -> 0 us
  blocking collectives: 222 us -> 0 us
  Pallas kernels: 0 us -> 107 us
  matrix products: 29.6 us -> 0 us
  starting transfers between devices: 29.1 us -> 0 us
  other arithmetic: 20 us -> 0 us
  between operations: 14.1 us -> 0.02 us
    psum x15 -> x0, waiting for transfers between devices: 863 us -> none  [the longest x5 416 us: backward_tick(): back_total = lax.psum(back_part, 'tensor')]
    psum x6 -> x0, blocking collectives: 222 us -> none  [the longest x5 157 us: forward_tick(): summed, square_total = lax.psum((partial_value, squares), 'tensor')]
    pallas_call x0 -> x1, Pallas kernels: none -> 107 us  [local(): pl.pallas_call(functools.partial(kernel, nd, nt, float(width)), out_shape...]
    reduce_scatter x2 -> x0, waiting for transfers between devices: 61.4 us -> none  [the longest x1 30.7 us: local(): lax.psum_scatter(lax.dot_general(partial_value, second_dirs, (((0,), (0,)...]
    all_gather x2 -> x0, waiting for transfers between devices: 45.1 us -> none  [the longest x1 25.7 us: local(): lax.all_gather(rotation.astype(jnp.bfloat16), 'dp', axis=0, tiled=True)]
    dot_general x26 -> x0, matrix products: 29.6 us -> none  [the longest x5 5.7 us: forward_tick(): jnp.dot(clipped, weight_out, preferred_element_type=jnp.float32)]
    ppermute x10 -> x0, starting transfers between devices: 28.6 us -> none  [from_behind(): return lax.ppermute(shard, axis, pairs)]
    ppermute x10 -> x0, waiting for transfers between devices: 15.3 us -> none  [from_behind(): return lax.ppermute(shard, axis, pairs)]
  transfers between devices with their start and end apart: 29 -> 0, of which waited for: 29 -> 0; matrix products, arithmetic and copies ran while one was open for 1% -> 0% of each run, Pallas kernels for 0% -> 0%
where the time goes in v1:
time: 114 us
  Pallas kernels  107 us (94%)
  local copies, waits for them, and re-layouts  6.49 us (6%)
    pallas_call x1, Pallas kernels, local(): pl.pallas_call(functools.partial(kernel, nd, nt, float(width)), out_shape...  107 us
    unnamed x13, local copies, waits for them, and re-layouts  6.49 us

profile of v1, /device:TPU:1, one launch (start us, length us, event | category | flops | bytes accessed | tf_op | source)
XLA Modules:
  0.0 113.9 jit_solution(6211693446772198687)
XLA Ops:
  0.0 0.0 copy-start
  0.0 1.0 copy-done
  1.0 0.0 copy-start.1
  1.0 1.0 copy-done.1
  2.1 0.0 copy-start.2
  2.1 1.0 copy-done.2
  3.1 0.0 copy-start.3
  3.1 1.0 copy-done.3
  4.2 0.0 copy-start.4
  4.2 0.8 copy-done.4
  5.0 0.0 copy-start.5
  5.0 0.7 copy-done.5
  5.7 107.4 %shard_map.64 = f32[512,256]{1,0:T(8,128)S(1)} custom-call(bf16[128,2048]{1,0:T(8,128)(2,1)S(1)} %copy-done, f32[512,256]{1,0:T(8,128)S(1)} %copy-done.1, bf16[1,256,1024]{2,1,0:T(8,128)(2,1)S(1)} %copy-done.2, bf16[1,1024,256]{2,1,0:T(8,128)(2,1)S(1)} %copy-done.3, s32[1,1024]{1,0:T(1,128)S(1)} %copy-done.5, bf16[128,256]{1,0:T(8,128)(2,1)S(1)} %copy-done.4), custom_call_target="tpu_custom_call" | custom-call | tf_op jit(solution)/shard_map/pallas_call | solution.py:451
  113.1 0.8 copy.8
Async XLA Ops:
  0.0 1.0 copy-start
  1.0 1.0 copy-start.1
  2.1 1.0 copy-start.2
  3.1 1.0 copy-start.3
  4.2 0.8 copy-start.4
  5.0 0.7 copy-start.5

commit v2 on v1

v2 whole, which is shorter than its diff:
```python
import functools
import math

import jax
import jax.numpy as jnp
from jax import lax
from jax.experimental import pallas as pl
from jax.experimental.pallas import tpu as pltpu
from jax.sharding import PartitionSpec as P

BF = jnp.bfloat16
F32 = jnp.float32
YT = jnp.float32
LANES = 128
NT_DIMS = (((1,), (1,)), ((), ()))


def dot(a, b):
    return jnp.dot(a, b, preferred_element_type=F32)


def dot_nt(a, b):
    return lax.dot_general(a, b, NT_DIMS, preferred_element_type=F32)


def up(a):
    return a.astype(F32)


def far_first(edge):
    cells = [(a, b) for a in range(edge) for b in range(edge) if a or b]
    return sorted(cells, key=lambda c: -min(c[0], edge - c[0]) - min(c[1], edge - c[1]))


def kernel(
    nd,
    nt,
    width,
    e_hbm,
    r_hbm,
    v_hbm,
    o_hbm,
    m_hbm,
    u_hbm,
    out_ref,
    e_ref,
    r_ref,
    v_ref,
    o_ref,
    m_ref,
    u_ref,
    rg,
    xpart,
    xrecv,
    xall,
    eall,
    gall,
    v1,
    bnd,
    bnd1,
    dcbuf,
    dc1recv,
    ybuf,
    y0recv,
    y1recv,
    cbuf,
    qbuf,
    dc0recv,
    q0buf,
    vpart,
    vrecv,
    vown,
    vall,
    gram,
    gramrecv,
    gramall,
    xgram,
    xgramrecv,
    xgramall,
    xx,
    yall,
    nsbuf,
    nsrecv,
    obuf,
    insem,
    tsend,
    trecv,
    rsend,
    rrecv,
    xsend,
    xrecv_sem,
    gsend,
    grecv,
    psend,
    precv,
):
    p = lax.axis_index("pipe")
    d = lax.axis_index("dp")
    t = lax.axis_index("tensor")
    tg = u_ref.shape[0]
    half = ybuf.shape[1] - LANES
    own = tg // (nt // 2)
    rows = rg.shape[1]
    group = 2 * nd
    slot = p * nd + d
    edge = math.isqrt(nt)
    tz, ty = t // edge, lax.rem(t, edge)
    tokens = nd * tg
    mine = tg // 2
    my_half = lax.rem(t, 2)

    def rcopy(src, dst, ssem, rsem, to):
        return pltpu.make_async_remote_copy(
            src_ref=src,
            dst_ref=dst,
            send_sem=ssem,
            recv_sem=rsem,
            device_id=to,
            device_id_type=pl.DeviceIdType.MESH,
        )

    others = []
    for a, b in far_first(edge):
        others.append(lax.rem(tz + a, edge) * edge + lax.rem(ty + b, edge))

    def to_plane(ph, src, dst):
        for i, j in enumerate(others):
            rcopy(src(j), dst(i), tsend.at[ph], trecv.at[ph], (p, d, j)).start()

    def plane_wait(ph, like):
        return rcopy(like, like, tsend.at[ph], trecv.at[ph], (p, d, others[-1]))

    def total(first, recv):
        acc = first.astype(F32)
        for i in range(nt - 1):
            acc = acc + recv[i].astype(F32)
        return acc

    def spot(j):
        return pl.ds(pl.multiple_of(lax.rem(j, 2) * tg + (j // 2) * own, own), own)

    def like(buf):
        return buf.at[pl.ds(0, (nt - 1) * own)]

    def rs_start(ph, buf, recv):
        to_plane(ph, lambda j: buf.at[spot(j)], lambda i: recv.at[i])

    def rs_total(ph, buf, recv):
        plane_wait(ph, recv).wait_recv()
        return total(buf[spot(t)], recv)

    def ag_start(ph, buf):
        to_plane(ph, lambda j: buf.at[spot(t)], lambda i: buf.at[spot(t)])

    def ag_wait(ph, buf):
        plane_wait(ph, like(buf)).wait_recv()

    def ring(k):
        return lax.rem(d + k, nd)

    partner = (1 - p, d, t)

    def to_ring(ph, src, dst):
        for k in (2, 1, 3):
            rcopy(src(ring(k)), dst(ring(k)), xsend.at[ph], xrecv_sem.at[ph], (p, ring(k), t)).start()

    def ring_wait(ph, like):
        return rcopy(like, like, xsend.at[ph], xrecv_sem.at[ph], (p, ring(1), t))

    loads = [
        pltpu.make_async_copy(src, dst, insem.at[i])
        for i, (src, dst) in enumerate(
            (
                (r_hbm, r_ref),
                (u_hbm, u_ref),
                (o_hbm, o_ref),
                (m_hbm, m_ref),
                (v_hbm, v_ref),
                (e_hbm, e_ref),
            )
        )
    ]
    for load in loads:
        load.start()

    bar = pltpu.get_barrier_semaphore()

    def greet(to):
        pl.semaphore_signal(bar, inc=1, device_id=to, device_id_type=pl.DeviceIdType.MESH)

    for j in others:
        greet((p, d, j))
    for k in range(1, nd):
        greet((p, ring(k), t))
        greet((1 - p, ring(k), t))
    greet(partner)

    loads[0].wait()
    rg[pl.ds(d, 1)] = (r_ref[...] * (1.0 / math.sqrt(width))).astype(BF)[None]
    pl.semaphore_wait(bar, nt - 1 + 2 * (nd - 1) + 1)

    hrow = rows // 2

    def r_half(s, h, to, i):
        blk = rg.at[s, pl.ds(h * hrow, hrow)]
        return rcopy(blk, blk, rsend.at[i], rrecv.at[i], (p, ring(to), t))

    ahead, behind = 1, nd - 1
    r_sends = [
        r_half(d, 0, ahead, 0),
        r_half(d, 1, behind, 1),
        r_half(d, 1, ahead, 2),
        r_half(d, 0, behind, 3),
    ]
    r_gets = [
        r_half(ring(behind), 0, ahead, 0),
        r_half(ring(ahead), 1, behind, 1),
        r_half(ring(behind), 1, ahead, 2),
        r_half(ring(ahead), 0, behind, 3),
    ]
    r_on = [r_half(ring(behind), 0, ahead, 4), r_half(ring(ahead), 1, behind, 5)]
    r_far = [r_half(ring(2), 0, ahead, 4), r_half(ring(2), 1, behind, 5)]
    for c in r_sends:
        c.start()
    for load in loads[1:]:
        load.wait()

    v1_copy = rcopy(v_ref.at[0], v1, psend.at[0], precv.at[0], partner)
    b1_copy = rcopy(bnd, bnd1, psend.at[1], precv.at[1], partner)
    d1_copy = rcopy(dcbuf, dcbuf, psend.at[2], precv.at[2], partner)
    x_copy = rcopy(xpart, xrecv, psend.at[3], precv.at[3], partner)
    xx_copy = rcopy(xgramall.at[0, pl.ds(0, mine)], xx, psend.at[4], precv.at[4], partner)
    g_copy = rcopy(gall.at[d], gall.at[d], psend.at[5], precv.at[5], partner)

    bnd[...] = jnp.broadcast_to(jnp.exp2(m_ref[...].astype(F32)), bnd.shape)

    def store_dc(part):
        dcbuf[:tg] = part[:, :half].astype(BF)
        dcbuf[tg:] = part[:, half:].astype(BF)

    @pl.when(p == 1)
    def _():
        store_dc(dot_nt(u_ref[...], o_ref[0]))
        d1_copy.start()
        b1_copy.start()
        v1_copy.start()

    @pl.when(p == 0)
    def _():
        d1_copy.wait_recv()
        rs_start(0, dcbuf, dc1recv)

    def e_dot(s):
        return dot(e_ref[:, pl.ds(pl.multiple_of(s * rows, LANES), rows)], rg[s])

    r_gets[0].wait_recv()
    r_on[0].start()
    r_gets[1].wait_recv()
    r_on[1].start()
    part = e_dot(d)
    r_gets[2].wait_recv()
    r_gets[3].wait_recv()
    part = part + e_dot(ring(1)) + e_dot(ring(3))
    r_far[0].wait_recv()
    r_far[1].wait_recv()
    part = part + e_dot(ring(2))
    xpart[...] = part.astype(BF)
    x_copy.start()
    x_copy.wait_recv()
    xall[pl.ds(d, 1)] = (up(xpart[...]) + up(xrecv[...])).astype(BF)[None]

    def share_inputs():
        to_ring(0, lambda j: xall.at[d], lambda j: xall.at[d])
        to_ring(
            1,
            lambda j: e_ref.at[:, pl.ds(pl.multiple_of(j * rows, LANES), rows)],
            lambda j: eall.at[d],
        )
        eall[pl.ds(d, 1)] = e_ref[:, pl.ds(pl.multiple_of(d * rows, LANES), rows)][None]

    gcol = tokens // edge

    def gspot(buf, j):
        grow = buf.shape[1] // edge
        return (
            slice(None),
            pl.ds(pl.multiple_of((j // edge) * grow, grow), grow),
            pl.ds(pl.multiple_of(lax.rem(j, edge) * gcol, gcol), gcol),
        )

    def gram_start(ph, buf, recv):
        to_plane(ph, lambda j: buf.at[gspot(buf, j)], lambda i: recv.at[i])

    def gram_turn(ph, buf, recv, full):
        plane_wait(ph, recv).wait_recv()
        full[gspot(full, t)] = total(buf[gspot(buf, t)], recv).astype(BF)
        blk = full.at[gspot(full, t)]
        to_plane(ph + 1, lambda j: blk, lambda i: blk)

    @pl.when(p == 0)
    def _():
        def two_parts(col):
            hi = up(col.astype(BF))
            shape = (col.shape[0], LANES)
            lane = lax.broadcasted_iota(jnp.int32, shape, 1)
            return jnp.where(lane < LANES // 2, jnp.broadcast_to(hi, shape), jnp.broadcast_to(col - hi, shape))

        def one_part(lanes):
            return jnp.sum(lanes, axis=1, keepdims=True) * (2.0 / LANES)

        def store_y(y, h):
            hf = up(h)
            sq = two_parts(jnp.sum(hf * hf, axis=1, keepdims=True)).astype(YT)
            ybuf[:tg, :half] = y[:, :half].astype(YT)
            ybuf[tg:, :half] = y[:, half:].astype(YT)
            ybuf[:tg, half:] = sq
            ybuf[tg:, half:] = sq

        def pick(b):
            return jnp.where(my_half == 0, b[0:1, :half], b[0:1, half:])

        def norm(tot):
            return lax.rsqrt(one_part(tot[:, half:]) / width + 1e-05)

        def gate(tot, dc, inv, bound, buf):
            y = tot[:, :half]
            z = inv * y
            inside = (z >= -8.0 * bound) & (z <= 7.0 * bound)
            q = (inv * jnp.where(inside, dc, 0.0)).astype(BF)
            coef = inv * inv / width * jnp.sum(up(q) * y, axis=1, keepdims=True)
            buf[spot(t), :half] = q
            buf[spot(t), half:] = two_parts(coef).astype(BF)

        def grad_in(buf, w):
            lin = dot_nt(buf[:tg, :half], w[:, :half]) + dot_nt(buf[tg:, :half], w[:, half:])
            return lin, one_part(up(buf[:tg, half:]) + up(buf[tg:, half:]))

        h0 = xall[d]
        store_y(dot(h0, v_ref[0]), h0)
        rs_start(1, ybuf, y0recv)
        share_inputs()
        tot0 = rs_total(1, ybuf, y0recv)
        inv0 = norm(tot0)
        bound0 = pick(bnd)
        cbuf[spot(t)] = jnp.clip(inv0 * tot0[:, :half], -8.0 * bound0, 7.0 * bound0).astype(BF)
        ag_start(2, cbuf)
        plane_wait(1, like(ybuf)).wait_send()
        ag_wait(2, cbuf)
        wo = o_ref[0]
        h1 = (up(xall[d]) + dot(cbuf[:tg], wo[:half]) + dot(cbuf[tg:], wo[half:])).astype(BF)
        v1_copy.wait_recv()
        b1_copy.wait_recv()
        store_y(dot(h1, v1[...]), h1)
        rs_start(3, ybuf, y1recv)
        dc1 = rs_total(0, dcbuf, dc1recv)
        plane_wait(0, like(dcbuf)).wait_send()
        tot1 = rs_total(3, ybuf, y1recv)
        gate(tot1, dc1, norm(tot1), pick(bnd1), qbuf)
        ag_start(4, qbuf)
        ag_wait(4, qbuf)
        lin, coef = grad_in(qbuf, v1[...])
        u1 = (up(u_ref[...]) + lin - coef * up(h1)).astype(BF)
        store_dc(dot_nt(u1, o_ref[0]))
        rs_start(5, dcbuf, dc0recv)
        dc0 = rs_total(5, dcbuf, dc0recv)
        gate(tot0, dc0, inv0, bound0, q0buf)
        ag_start(6, q0buf)
        ag_wait(6, q0buf)
        lin, coef = grad_in(q0buf, v_ref[0])
        gall[pl.ds(d, 1)] = (up(u1) + lin - coef * up(xall[d])).astype(BF)[None]
        g_copy.start()
        for i in range(2):
            for k in (2, 1, 3):
                rcopy(gall.at[d], gall.at[d], gsend.at[i], grecv.at[i], (i, ring(k), t)).start()

    @pl.when(p == 1)
    def _():
        share_inputs()
        ring_wait(0, xall.at[pl.ds(0, nd - 1)]).wait_recv()
        xgram[0] = dot_nt(xall[d], xall[...].reshape(tokens, xall.shape[2])).astype(BF)
        gram_start(10, xgram, xgramrecv)
        gram_turn(10, xgram, xgramrecv, xgramall)
        plane_wait(11, xgramrecv).wait_recv()
        xx[...] = xgramall[0, pl.ds(mine, mine)]
        xx_copy.start()
        g_copy.wait_recv()

    vsum = dot_nt(rg[...].reshape(nd * rows, rg.shape[2]), gall[d]).astype(BF)
    vpart[...] = vsum.reshape(nd, rows, tg)
    vrow = rows // nt

    def vspot(j):
        return pl.ds(pl.multiple_of(j * vrow, vrow), vrow)

    to_plane(7, lambda j: vpart.at[:, vspot(j)], lambda i: vrecv.at[i])

    my_rows = pl.ds(pl.multiple_of(p * mine, mine), mine)
    g_three = gall.at[pl.ds(0, nd - 1)]

    @pl.when(p == 0)
    def _():
        ring_wait(0, xall.at[pl.ds(0, nd - 1)]).wait_recv()
        rcopy(g_three, g_three, gsend.at[0], grecv.at[0], partner).wait_recv()

    @pl.when(p == 1)
    def _():
        rcopy(g_three, g_three, gsend.at[1], grecv.at[1], partner).wait_recv()

    hid = xall[...].reshape(tokens, xall.shape[2])
    g_mine = gall[d, my_rows]
    x_mine = xall[d, my_rows]
    grad = gall[...].reshape(tokens, gall.shape[2])
    gram[0] = dot_nt(g_mine, hid).astype(BF)
    gram[1] = dot_nt(g_mine, grad).astype(BF)
    gram[2] = dot_nt(x_mine, grad).astype(BF)
    gram_start(8, gram, gramrecv)

    plane_wait(7, vrecv).wait_recv()
    vown[...] = total(vpart[:, vspot(t)], vrecv).astype(BF)
    vmine = (vspot(t), pl.ds(pl.multiple_of(d * tg, tg), tg))
    to_ring(2, lambda j: vown.at[j], lambda j: vall.at[vmine])
    vall[vmine] = vown[d]

    gram_turn(8, gram, gramrecv, gramall)
    v_three = vown.at[pl.ds(0, nd - 1)]
    ring_wait(2, v_three).wait_recv()
    to_plane(12, lambda j: vall.at[vspot(t)], lambda i: vall.at[vspot(t)])

    e_three = eall.at[pl.ds(0, nd - 1)]
    ring_wait(1, e_three).wait_recv()
    emb_t = eall[...].reshape(tokens, rows).T
    front = 2.0 * dot(emb_t, grad)

    @pl.when(p == 0)
    def _():
        xx_copy.wait_recv()

    plane_wait(9, gramrecv).wait_recv()
    g_x, g_g, x_g, x_x = gramall[0], gramall[1], gramall[2], xx[...]

    def to_group(ph, src, dst):
        for k in (6, 2, 5, 7, 1, 3, 4):
            j = lax.rem(slot + k, group)
            rcopy(src, dst(k), gsend.at[ph], grecv.at[ph], (j // nd, lax.rem(j, nd), t)).start()

    def group_wait(ph, like):
        return rcopy(like, like, gsend.at[ph], grecv.at[ph], partner)

    nsbuf[...] = jnp.broadcast_to(8.0 * jnp.sum(up(x_x) * up(g_g) - up(g_x) * up(x_g)), nsbuf.shape)
    to_group(2, nsbuf, lambda k: nsrecv.at[k - 1])
    place = d * 2 + p
    yall[place, 0] = (2.0 * (dot(g_x, grad) - dot(g_g, hid))).astype(BF)
    yall[place, 1] = (2.0 * (dot(x_g, hid) - dot(x_x, grad))).astype(BF)
    to_group(3, yall.at[place], lambda k: yall.at[place])

    v_like = vall.at[pl.ds(0, (nt - 1) * vrow)]
    plane_wait(12, v_like).wait_recv()
    vt = vall[...]
    front = front - 2.0 * dot(vt, hid)
    group_wait(2, nsrecv).wait_recv()
    ns = nsbuf[...]
    for k in range(group - 1):
        ns = ns + nsrecv[k]
    rate = jnp.sqrt(width / (ns[0:1, 0:1] + 1e-06))
    scale = math.sqrt(width)
    obuf[...] = r_ref[...] - (0.5 * scale) * rate * front
    y_like = yall.at[pl.ds(0, group - 1)]
    group_wait(3, y_like).wait_recv()
    ya = yall[:, 0].reshape(tokens, -1)
    yb = yall[:, 1].reshape(tokens, -1)
    outs = []
    cut = rows // 4
    for i in range(4):
        blk = slice(i * cut, (i + 1) * cut)
        last = dot(emb_t[blk], ya) + dot(vt[blk], yb)
        obuf[blk] = obuf[blk] + (0.25 * scale) * (rate * rate) * last
        c = pltpu.make_async_copy(obuf.at[pl.ds(i * cut, cut)], out_ref.at[pl.ds(i * cut, cut)], insem.at[i])
        c.start()
        outs.append(c)

    for c in r_sends + r_on:
        c.wait_send()
    x_copy.wait_send()
    ring_wait(0, xall.at[pl.ds(0, nd - 1)]).wait_send()
    ring_wait(1, e_three).wait_send()
    ring_wait(2, v_three).wait_send()

    @pl.when(p == 0)
    def _():
        plane_wait(2, like(cbuf)).wait_send()
        plane_wait(3, like(ybuf)).wait_send()
        plane_wait(4, like(qbuf)).wait_send()
        plane_wait(5, like(dcbuf)).wait_send()
        plane_wait(6, like(q0buf)).wait_send()
        g_copy.wait_send()
        rcopy(g_three, g_three, gsend.at[0], grecv.at[0], partner).wait_send()
        rcopy(g_three, g_three, gsend.at[1], grecv.at[1], partner).wait_send()

    @pl.when(p == 1)
    def _():
        d1_copy.wait_send()
        b1_copy.wait_send()
        v1_copy.wait_send()
        plane_wait(10, xgramrecv).wait_send()
        plane_wait(11, xgramrecv).wait_send()
        xx_copy.wait_send()

    plane_wait(7, vrecv).wait_send()
    plane_wait(8, gramrecv).wait_send()
    plane_wait(9, gramrecv).wait_send()
    plane_wait(12, v_like).wait_send()
    group_wait(2, nsrecv).wait_send()
    group_wait(3, y_like).wait_send()
    for c in outs:
        c.wait()


def solution(mesh):
    nd = mesh.shape["dp"]
    nt = mesh.shape["tensor"]

    def local(embedded, rotation, value_proj, output_proj, mid_exponent, cotangent):
        tg = embedded.shape[0]
        rows, cols = rotation.shape
        width = cols * nt
        units = value_proj.shape[2]
        half = units // 2
        own = tg // (nt // 2)
        group = 2 * nd
        edge = math.isqrt(nt)
        mine = tg // 2
        tokens = nd * tg
        vm = pltpu.VMEM
        dma = pltpu.SemaphoreType.DMA
        scratch = [
            vm(embedded.shape, BF),
            vm(rotation.shape, F32),
            vm(value_proj.shape, BF),
            vm(output_proj.shape, BF),
            vm(mid_exponent.shape, jnp.int32),
            vm(cotangent.shape, BF),
            vm((nd, rows, cols), BF),
            vm((tg, cols), BF),
            vm((tg, cols), BF),
            vm((nd, tg, cols), BF),
            vm((nd, tg, rows), BF),
            vm((nd, tg, cols), BF),
            vm((cols, units), BF),
            vm((8, units), F32),
            vm((8, units), F32),
            vm((2 * tg, half), BF),
            vm((nt - 1, own, half), BF),
            vm((2 * tg, half + LANES), YT),
            vm((nt - 1, own, half + LANES), YT),
            vm((nt - 1, own, half + LANES), YT),
            vm((2 * tg, half), BF),
            vm((2 * tg, half + LANES), BF),
            vm((nt - 1, own, half), BF),
            vm((2 * tg, half + LANES), BF),
            vm((nd, rows, tg), BF),
            vm((nt - 1, nd, rows // nt, tg), BF),
            vm((nd, rows // nt, tg), BF),
            vm((rows, tokens), BF),
            vm((3, mine, tokens), BF),
            vm((nt - 1, 3, mine // edge, tokens // edge), BF),
            vm((3, mine, tokens), BF),
            vm((1, tg, tokens), BF),
            vm((nt - 1, 1, tg // edge, tokens // edge), BF),
            vm((1, tg, tokens), BF),
            vm((mine, tokens), BF),
            vm((group, 2, mine, cols), BF),
            vm((8, LANES), F32),
            vm((group - 1, 8, LANES), F32),
            vm((rows, cols), F32),
            dma((6,)),
            dma((13,)),
            dma((13,)),
            dma((6,)),
            dma((6,)),
            dma((3,)),
            dma((3,)),
            dma((4,)),
            dma((4,)),
            dma((6,)),
            dma((6,)),
        ]
        return pl.pallas_call(
            functools.partial(kernel, nd, nt, float(width)),
            out_shape=jax.ShapeDtypeStruct((rows, cols), F32),
            in_specs=[pl.BlockSpec(memory_space=pltpu.HBM)] * 6,
            out_specs=pl.BlockSpec(memory_space=pltpu.HBM),
            scratch_shapes=scratch,
            compiler_params=pltpu.CompilerParams(
                collective_id=0, has_side_effects=True, vmem_limit_bytes=67043328
            ),
        )(embedded, rotation, value_proj, output_proj, mid_exponent, cotangent)

    return jax.shard_map(
        local,
        mesh=mesh,
        in_specs=(
            P("dp", "pipe"),
            P(("pipe", "dp"), "tensor"),
            P("pipe", "tensor", None),
            P("pipe", None, "tensor"),
            P("pipe", None),
            P("dp", "tensor"),
        ),
        out_specs=P(("pipe", "dp"), "tensor"),
        check_vma=False,
    )
```

time: 114 us -> 86.6 us (0.76)
  Pallas kernels: 107 us -> 84.6 us
  local copies, waits for them, and re-layouts: 6.49 us -> 1.87 us
    pallas_call x1, Pallas kernels: 107 us -> 84.6 us  [local(): pl.pallas_call(functools.partial(kernel, nd, nt, float(width)), out_shape...]
    unnamed x13 -> x1, local copies, waits for them, and re-layouts: 6.49 us -> 1.87 us
where the time goes in v2:
time: 86.6 us; the launch traced here: 86.5 us
  Pallas kernels  84.6 us (98%)
  local copies, waits for them, and re-layouts  1.87 us (2%)
    pallas_call x1, Pallas kernels, local(): pl.pallas_call(functools.partial(kernel, nd, nt, float(width)), out_shape...  84.6 us
    unnamed x1, local copies, waits for them, and re-layouts  1.87 us

profile of v2, /device:TPU:1, one launch (start us, length us, event | category | flops | bytes accessed | tf_op | source)
XLA Modules:
  0.0 86.5 jit_solution(17532700596017818424)
XLA Ops:
  0.0 84.6 %shard_map.64 = f32[512,256]{1,0:T(8,128)} custom-call(bf16[128,2048]{1,0:T(8,128)(2,1)} %e_hbm.1, f32[512,256]{1,0:T(8,128)} %r_hbm.1, bf16[1,256,1024]{2,1,0:T(8,128)(2,1)} %v_hbm.1, bf16[1,1024,256]{2,1,0:T(8,128)(2,1)} %o_hbm.1, s32[1,1024]{1,0:T(1,128)} %m_hbm.1, bf16[128,256]{1,0:T(8,128)(2,1)} %u_hbm.1), custom_call_target="tpu_custom_call" | custom-call | tf_op jit(solution)/shard_map/pallas_call | solution.py:587
  84.6 1.9 %copy.8 = f32[512,256]{1,0:T(8,128)} copy(f32[512,256]{1,0:T(8,128)} %shard_map.64) | data formatting | bytes 1048576

commit v3 on v2

--- a/solution.py
+++ b/solution.py
@@ -60,12 +60,18 @@
     bnd1,
     dcbuf,
     dc1recv,
+    e2buf,
+    e2recv,
+    hobuf,
+    horecv,
+    pbuf,
+    pbrecv,
+    pall,
     ybuf,
     y0recv,
     y1recv,
     cbuf,
     qbuf,
-    dc0recv,
     q0buf,
     vpart,
     vrecv,
@@ -98,8 +104,8 @@
     d = lax.axis_index("dp")
     t = lax.axis_index("tensor")
     tg = u_ref.shape[0]
-    half = ybuf.shape[1] - LANES
-    own = tg // (nt // 2)
+    span = ybuf.shape[2]
+    own = tg // 2
     rows = rg.shape[1]
     group = 2 * nd
     slot = p * nd + d
@@ -107,7 +113,7 @@
     tz, ty = t // edge, lax.rem(t, edge)
     tokens = nd * tg
     mine = tg // 2
-    my_half = lax.rem(t, 2)
+    my_side = lax.rem(t, 2)
 
     def rcopy(src, dst, ssem, rsem, to):
         return pltpu.make_async_remote_copy(
@@ -136,21 +142,29 @@
             acc = acc + recv[i].astype(F32)
         return acc
 
-    def spot(j):
-        return pl.ds(pl.multiple_of(lax.rem(j, 2) * tg + (j // 2) * own, own), own)
+    def split(buf, y):
+        for j in range(nt):
+            i, g = j % 2, j // 2
+            buf[j, :own] = y[i * own : (i + 1) * own, g * span : (g + 1) * span].astype(buf.dtype)
+
+    def side_of(buf, i):
+        return jnp.concatenate([buf[2 * g + i, :own] for g in range(nt // 2)], axis=1)
+
+    def join(buf):
+        return jnp.concatenate([side_of(buf, 0), side_of(buf, 1)], axis=0)
 
     def like(buf):
-        return buf.at[pl.ds(0, (nt - 1) * own)]
+        return buf.at[pl.ds(0, nt - 1)]
 
     def rs_start(ph, buf, recv):
-        to_plane(ph, lambda j: buf.at[spot(j)], lambda i: recv.at[i])
+        to_plane(ph, lambda j: buf.at[j], lambda i: recv.at[i])
 
     def rs_total(ph, buf, recv):
         plane_wait(ph, recv).wait_recv()
-        return total(buf[spot(t)], recv)
+        return total(buf[t], recv)
 
     def ag_start(ph, buf):
-        to_plane(ph, lambda j: buf.at[spot(t)], lambda i: buf.at[spot(t)])
+        to_plane(ph, lambda j: buf.at[t], lambda i: buf.at[t])
 
     def ag_wait(ph, buf):
         plane_wait(ph, like(buf)).wait_recv()
@@ -234,19 +248,22 @@
 
     bnd[...] = jnp.broadcast_to(jnp.exp2(m_ref[...].astype(F32)), bnd.shape)
 
-    def store_dc(part):
-        dcbuf[:tg] = part[:, :half].astype(BF)
-        dcbuf[tg:] = part[:, half:].astype(BF)
-
     @pl.when(p == 1)
     def _():
-        store_dc(dot_nt(u_ref[...], o_ref[0]))
+        v1_copy.start()
+        split(dcbuf, dot_nt(u_ref[...], o_ref[0]))
         d1_copy.start()
         b1_copy.start()
-        v1_copy.start()
 
     @pl.when(p == 0)
     def _():
+        split(e2buf, dot_nt(u_ref[...], o_ref[0]))
+        v1_copy.wait_recv()
+        quarter = pbuf.shape[2]
+        cross = dot(o_ref[0], v1[:, pl.ds(pl.multiple_of(d * quarter, quarter), quarter)])
+        pbuf[...] = cross.astype(BF).reshape(pbuf.shape)
+        to_plane(13, lambda j: pbuf.at[j // 2], lambda i: pbrecv.at[i])
+        rs_start(5, e2buf, e2recv)
         d1_copy.wait_recv()
         rs_start(0, dcbuf, dc1recv)
 
@@ -299,72 +316,95 @@
 
     @pl.when(p == 0)
     def _():
-        def two_parts(col):
-            hi = up(col.astype(BF))
-            shape = (col.shape[0], LANES)
-            lane = lax.broadcasted_iota(jnp.int32, shape, 1)
-            return jnp.where(lane < LANES // 2, jnp.broadcast_to(hi, shape), jnp.broadcast_to(col - hi, shape))
-
-        def one_part(lanes):
-            return jnp.sum(lanes, axis=1, keepdims=True) * (2.0 / LANES)
+        def diagonal():
+            shape = (own, LANES)
+            return lax.broadcasted_iota(jnp.int32, shape, 0) == lax.broadcasted_iota(jnp.int32, shape, 1)
+
+        def to_row(col):
+            return jnp.sum(jnp.where(diagonal(), col, 0.0), axis=0, keepdims=True)
+
+        def to_col(row):
+            return jnp.sum(jnp.where(diagonal(), row, 0.0), axis=1, keepdims=True)
 
         def store_y(y, h):
+            split(ybuf, y)
             hf = up(h)
-            sq = two_parts(jnp.sum(hf * hf, axis=1, keepdims=True)).astype(YT)
-            ybuf[:tg, :half] = y[:, :half].astype(YT)
-            ybuf[tg:, :half] = y[:, half:].astype(YT)
-            ybuf[:tg, half:] = sq
-            ybuf[tg:, half:] = sq
+            sq = jnp.sum(hf * hf, axis=1, keepdims=True)
+            for i in range(2):
+                tile = jnp.broadcast_to(to_row(sq[i * own : (i + 1) * own]), (8, LANES))
+                for g in range(nt // 2):
+                    ybuf[2 * g + i, own:] = tile
 
         def pick(b):
-            return jnp.where(my_half == 0, b[0:1, :half], b[0:1, half:])
+            g = t // 2
+            out = b[0:1, :span]
+            for i in range(1, nt // 2):
+                out = jnp.where(g == i, b[0:1, i * span : (i + 1) * span], out)
+            return out
 
         def norm(tot):
-            return lax.rsqrt(one_part(tot[:, half:]) / width + 1e-05)
+            return lax.rsqrt(to_col(tot[own : own + 1]) / width + 1e-05)
 
         def gate(tot, dc, inv, bound, buf):
-            y = tot[:, :half]
+            y = tot[:own]
             z = inv * y
             inside = (z >= -8.0 * bound) & (z <= 7.0 * bound)
             q = (inv * jnp.where(inside, dc, 0.0)).astype(BF)
-            coef = inv * inv / width * jnp.sum(up(q) * y, axis=1, keepdims=True)
-            buf[spot(t), :half] = q
-            buf[spot(t), half:] = two_parts(coef).astype(BF)
+            coef = to_row(inv * inv / width * jnp.sum(up(q) * y, axis=1, keepdims=True))
+            hi = up(coef.astype(BF))
+            row = lax.broadcasted_iota(jnp.int32, (16, LANES), 0)
+            buf[t, :own] = q
+            buf[t, own:] = jnp.where(row == 0, hi, jnp.where(row == 1, coef - hi, 0.0)).astype(BF)
+
+        def coef_of(buf, i):
+            ext = up(buf[i, own:])
+            for g in range(1, nt // 2):
+                ext = ext + up(buf[2 * g + i, own:])
+            return to_col(jnp.sum(ext, axis=0, keepdims=True))
 
         def grad_in(buf, w):
-            lin = dot_nt(buf[:tg, :half], w[:, :half]) + dot_nt(buf[tg:, :half], w[:, half:])
-            return lin, one_part(up(buf[:tg, half:]) + up(buf[tg:, half:]))
+            coef = jnp.concatenate([coef_of(buf, 0), coef_of(buf, 1)], axis=0)
+            return dot_nt(join(buf), w), coef
 
         h0 = xall[d]
         store_y(dot(h0, v_ref[0]), h0)
         rs_start(1, ybuf, y0recv)
         share_inputs()
+        plane_wait(13, pbrecv).wait_recv()
+        pall[pl.ds(d, 1)] = total(pbuf[t // 2], pbrecv).astype(BF)[None]
+        to_ring(3, lambda j: pall.at[d], lambda j: pall.at[d])
         tot0 = rs_total(1, ybuf, y0recv)
         inv0 = norm(tot0)
         bound0 = pick(bnd)
-        cbuf[spot(t)] = jnp.clip(inv0 * tot0[:, :half], -8.0 * bound0, 7.0 * bound0).astype(BF)
+        cbuf[t] = jnp.clip(inv0 * tot0[:own], -8.0 * bound0, 7.0 * bound0).astype(BF)
         ag_start(2, cbuf)
         plane_wait(1, like(ybuf)).wait_send()
+        dc1 = rs_total(0, dcbuf, dc1recv)
+        e2 = rs_total(5, e2buf, e2recv)
+        b1_copy.wait_recv()
+        bound1 = pick(bnd1)
         ag_wait(2, cbuf)
-        wo = o_ref[0]
-        h1 = (up(xall[d]) + dot(cbuf[:tg], wo[:half]) + dot(cbuf[tg:], wo[half:])).astype(BF)
-        v1_copy.wait_recv()
-        b1_copy.wait_recv()
+        h1 = (up(xall[d]) + dot(join(cbuf), o_ref[0])).astype(BF)
         store_y(dot(h1, v1[...]), h1)
         rs_start(3, ybuf, y1recv)
-        dc1 = rs_total(0, dcbuf, dc1recv)
-        plane_wait(0, like(dcbuf)).wait_send()
+        split(hobuf, dot_nt(h1, o_ref[0]))
+        rs_start(14, hobuf, horecv)
         tot1 = rs_total(3, ybuf, y1recv)
-        gate(tot1, dc1, norm(tot1), pick(bnd1), qbuf)
+        gate(tot1, dc1, norm(tot1), bound1, qbuf)
         ag_start(4, qbuf)
+        ho = rs_total(14, hobuf, horecv)
+        p_three = pall.at[pl.ds(0, nd - 1)]
+        ring_wait(3, p_three).wait_recv()
         ag_wait(4, qbuf)
+        q1 = side_of(qbuf, my_side)
+        quarter = pall.shape[2]
+        dc0 = e2 - coef_of(qbuf, my_side) * ho
+        for i in range(nd):
+            dc0 = dc0 + dot_nt(q1[:, i * quarter : (i + 1) * quarter], pall[i])
+        gate(tot0, dc0, inv0, bound0, q0buf)
+        ag_start(6, q0buf)
         lin, coef = grad_in(qbuf, v1[...])
         u1 = (up(u_ref[...]) + lin - coef * up(h1)).astype(BF)
-        store_dc(dot_nt(u1, o_ref[0]))
-        rs_start(5, dcbuf, dc0recv)
-        dc0 = rs_total(5, dcbuf, dc0recv)
-        gate(tot0, dc0, inv0, bound0, q0buf)
-        ag_start(6, q0buf)
         ag_wait(6, q0buf)
         lin, coef = grad_in(q0buf, v_ref[0])
         gall[pl.ds(d, 1)] = (up(u1) + lin - coef * up(xall[d])).astype(BF)[None]
@@ -487,11 +527,15 @@
 
     @pl.when(p == 0)
     def _():
+        plane_wait(0, like(dcbuf)).wait_send()
         plane_wait(2, like(cbuf)).wait_send()
         plane_wait(3, like(ybuf)).wait_send()
         plane_wait(4, like(qbuf)).wait_send()
-        plane_wait(5, like(dcbuf)).wait_send()
+        plane_wait(5, like(e2buf)).wait_send()
         plane_wait(6, like(q0buf)).wait_send()
+        plane_wait(13, pbrecv).wait_send()
+        plane_wait(14, like(hobuf)).wait_send()
+        ring_wait(3, pall.at[pl.ds(0, nd - 1)]).wait_send()
         g_copy.wait_send()
         rcopy(g_three, g_three, gsend.at[0], grecv.at[0], partner).wait_send()
         rcopy(g_three, g_three, gsend.at[1], grecv.at[1], partner).wait_send()
@@ -524,8 +568,8 @@
         rows, cols = rotation.shape
         width = cols * nt
         units = value_proj.shape[2]
-        half = units // 2
-        own = tg // (nt // 2)
+        own = tg // 2
+        span = units // (nt // 2)
         group = 2 * nd
         edge = math.isqrt(nt)
         mine = tg // 2
@@ -548,15 +592,21 @@
             vm((cols, units), BF),
             vm((8, units), F32),
             vm((8, units), F32),
-            vm((2 * tg, half), BF),
-            vm((nt - 1, own, half), BF),
-            vm((2 * tg, half + LANES), YT),
-            vm((nt - 1, own, half + LANES), YT),
-            vm((nt - 1, own, half + LANES), YT),
-            vm((2 * tg, half), BF),
-            vm((2 * tg, half + LANES), BF),
-            vm((nt - 1, own, half), BF),
-            vm((2 * tg, half + LANES), BF),
+            vm((nt, own, span), BF),
+            vm((nt - 1, own, span), BF),
+            vm((nt, own, span), BF),
+            vm((nt - 1, own, span), BF),
+            vm((nt, own, span), BF),
+            vm((nt - 1, own, span), BF),
+            vm((nt // 2, span, units // nd), BF),
+            vm((nt - 1, span, units // nd), BF),
+            vm((nd, span, units // nd), BF),
+            vm((nt, own + 8, span), YT),
+            vm((nt - 1, own + 8, span), YT),
+            vm((nt - 1, own + 8, span), YT),
+            vm((nt, own, span), BF),
+            vm((nt, own + 16, span), BF),
+            vm((nt, own + 16, span), BF),
             vm((nd, rows, tg), BF),
             vm((nt - 1, nd, rows // nt, tg), BF),
             vm((nd, rows // nt, tg), BF),
@@ -573,12 +623,12 @@
             vm((group - 1, 8, LANES), F32),
             vm((rows, cols), F32),
             dma((6,)),
-            dma((13,)),
-            dma((13,)),
-            dma((6,)),
-            dma((6,)),
-            dma((3,)),
-            dma((3,)),
+            dma((15,)),
+            dma((15,)),
+            dma((12,)),
+            dma((12,)),
+            dma((4,)),
+            dma((4,)),
             dma((4,)),
             dma((4,)),
             dma((6,)),

time: 86.6 us -> 80.9 us (0.934)
  Pallas kernels: 84.6 us -> 78.9 us
    pallas_call x1, Pallas kernels: 84.6 us -> 78.9 us  [local(): pl.pallas_call(functools.partial(kernel, nd, nt, float(width)), out_shape...]
where the time goes in v3:
time: 80.9 us; the launch traced here: 80.7 us
  Pallas kernels  78.9 us (98%)
  local copies, waits for them, and re-layouts  1.87 us (2%)
    pallas_call x1, Pallas kernels, local(): pl.pallas_call(functools.partial(kernel, nd, nt, float(width)), out_shape...  78.9 us
    unnamed x1, local copies, waits for them, and re-layouts  1.87 us

profile of v3, /device:TPU:1, one launch (start us, length us, event | category | flops | bytes accessed | tf_op | source)
XLA Modules:
  0.0 80.7 jit_solution(12669050766815184160)
XLA Ops:
  0.0 78.9 %shard_map.64 = f32[512,256]{1,0:T(8,128)} custom-call(bf16[128,2048]{1,0:T(8,128)(2,1)} %e_hbm.1, f32[512,256]{1,0:T(8,128)} %r_hbm.1, bf16[1,256,1024]{2,1,0:T(8,128)(2,1)} %v_hbm.1, bf16[1,1024,256]{2,1,0:T(8,128)(2,1)} %o_hbm.1, s32[1,1024]{1,0:T(1,128)} %m_hbm.1, bf16[128,256]{1,0:T(8,128)(2,1)} %u_hbm.1), custom_call_target="tpu_custom_call" | custom-call | tf_op jit(solution)/shard_map/pallas_call | solution.py:637
  78.9 1.9 %copy.8 = f32[512,256]{1,0:T(8,128)} copy(f32[512,256]{1,0:T(8,128)} %shard_map.64) | data formatting | bytes 1048576

commit v4 on v3

--- a/solution.py
+++ b/solution.py
@@ -11,6 +11,7 @@
 BF = jnp.bfloat16
 F32 = jnp.float32
 YT = jnp.float32
+OT = jnp.float32
 LANES = 128
 NT_DIMS = (((1,), (1,)), ((), ()))
 
@@ -87,7 +88,6 @@
     yall,
     nsbuf,
     nsrecv,
-    obuf,
     insem,
     tsend,
     trecv,
@@ -99,6 +99,10 @@
     grecv,
     psend,
     precv,
+    ysend,
+    yrecv,
+    vasend,
+    varecv,
 ):
     p = lax.axis_index("pipe")
     d = lax.axis_index("dp")
@@ -457,24 +461,45 @@
 
     plane_wait(7, vrecv).wait_recv()
     vown[...] = total(vpart[:, vspot(t)], vrecv).astype(BF)
-    vmine = (vspot(t), pl.ds(pl.multiple_of(d * tg, tg), tg))
+    vmine = (tz, ty, slice(None), pl.ds(pl.multiple_of(d * tg, tg), tg))
+
+    def v_turn(step):
+        cut = tokens // 2
+        lo, hi = pl.ds(0, cut), pl.ds(cut, cut)
+        if step == 0:
+            along_y, along_z = vall.at[tz, ty, :, lo], vall.at[tz, ty, :, hi]
+        else:
+            along_y, along_z = vall.at[:, ty, :, hi], vall.at[tz, :, :, lo]
+        for k in (2, 1, 3):
+            to_y = (p, d, tz * edge + lax.rem(ty + k, edge))
+            to_z = (p, d, lax.rem(tz + k, edge) * edge + ty)
+            rcopy(along_y, along_y, vasend.at[step, 0], varecv.at[step, 0], to_y).start()
+            rcopy(along_z, along_z, vasend.at[step, 1], varecv.at[step, 1], to_z).start()
+
+    def v_waits(step):
+        one = pl.ds(0, tokens // 2)
+        blk = vall.at[0, pl.ds(0, edge - 1), :, one] if step == 0 else vall.at[pl.ds(0, edge - 1), :, :, one]
+        return [rcopy(blk, blk, vasend.at[step, i], varecv.at[step, i], partner) for i in range(2)]
+
     to_ring(2, lambda j: vown.at[j], lambda j: vall.at[vmine])
     vall[vmine] = vown[d]
 
     gram_turn(8, gram, gramrecv, gramall)
     v_three = vown.at[pl.ds(0, nd - 1)]
     ring_wait(2, v_three).wait_recv()
-    to_plane(12, lambda j: vall.at[vspot(t)], lambda i: vall.at[vspot(t)])
+    v_turn(0)
 
     e_three = eall.at[pl.ds(0, nd - 1)]
     ring_wait(1, e_three).wait_recv()
     emb_t = eall[...].reshape(tokens, rows).T
-    front = 2.0 * dot(emb_t, grad)
 
     @pl.when(p == 0)
     def _():
         xx_copy.wait_recv()
 
+    for c in v_waits(0):
+        c.wait_recv()
+    v_turn(1)
     plane_wait(9, gramrecv).wait_recv()
     g_x, g_g, x_g, x_x = gramall[0], gramall[1], gramall[2], xx[...]
 
@@ -489,34 +514,44 @@
     nsbuf[...] = jnp.broadcast_to(8.0 * jnp.sum(up(x_x) * up(g_g) - up(g_x) * up(x_g)), nsbuf.shape)
     to_group(2, nsbuf, lambda k: nsrecv.at[k - 1])
     place = d * 2 + p
+
+    def y_ring(k, to):
+        blk = yall.at[lax.rem(d + to, nd) * 2 + p]
+        return rcopy(blk, blk, ysend.at[k], yrecv.at[k], (p, ring(k), t))
+
+    def y_chip(i):
+        blk = yall.at[i]
+        return rcopy(blk, blk, ysend.at[0], yrecv.at[0], partner)
+
     yall[place, 0] = (2.0 * (dot(g_x, grad) - dot(g_g, hid))).astype(BF)
     yall[place, 1] = (2.0 * (dot(x_g, hid) - dot(x_x, grad))).astype(BF)
-    to_group(3, yall.at[place], lambda k: yall.at[place])
-
-    v_like = vall.at[pl.ds(0, (nt - 1) * vrow)]
-    plane_wait(12, v_like).wait_recv()
-    vt = vall[...]
-    front = front - 2.0 * dot(vt, hid)
+    for k in (2, 1, 3):
+        y_ring(k, 0).start()
+    y_chip(place).start()
+
+    for c in v_waits(1):
+        c.wait_recv()
+    vt = vall[...].reshape(rows, tokens)
     group_wait(2, nsrecv).wait_recv()
     ns = nsbuf[...]
     for k in range(group - 1):
         ns = ns + nsrecv[k]
     rate = jnp.sqrt(width / (ns[0:1, 0:1] + 1e-06))
     scale = math.sqrt(width)
-    obuf[...] = r_ref[...] - (0.5 * scale) * rate * front
-    y_like = yall.at[pl.ds(0, group - 1)]
-    group_wait(3, y_like).wait_recv()
-    ya = yall[:, 0].reshape(tokens, -1)
-    yb = yall[:, 1].reshape(tokens, -1)
-    outs = []
+    for k in (1, 3, 2):
+        y_ring(k, nd - k).wait_recv()
+        y_chip(lax.rem(d + nd - k, nd) * 2 + p).start()
+    y_like = yall.at[pl.ds(0, nd)]
+    y_all = rcopy(y_like, y_like, ysend.at[0], yrecv.at[0], partner)
+    y_all.wait_recv()
+    half_rate = -0.5 * rate
+    za = (2.0 * up(grad) + half_rate * up(yall[:, 0].reshape(tokens, -1))).astype(BF)
+    zb = (-2.0 * up(hid) + half_rate * up(yall[:, 1].reshape(tokens, -1))).astype(BF)
     cut = rows // 4
     for i in range(4):
         blk = slice(i * cut, (i + 1) * cut)
-        last = dot(emb_t[blk], ya) + dot(vt[blk], yb)
-        obuf[blk] = obuf[blk] + (0.25 * scale) * (rate * rate) * last
-        c = pltpu.make_async_copy(obuf.at[pl.ds(i * cut, cut)], out_ref.at[pl.ds(i * cut, cut)], insem.at[i])
-        c.start()
-        outs.append(c)
+        last = dot(emb_t[blk], za) + dot(vt[blk], zb)
+        out_ref[blk] = r_ref[blk] - (0.5 * scale) * rate * last
 
     for c in r_sends + r_on:
         c.wait_send()
@@ -552,11 +587,13 @@
     plane_wait(7, vrecv).wait_send()
     plane_wait(8, gramrecv).wait_send()
     plane_wait(9, gramrecv).wait_send()
-    plane_wait(12, v_like).wait_send()
+    for step in range(2):
+        for c in v_waits(step):
+            c.wait_send()
     group_wait(2, nsrecv).wait_send()
-    group_wait(3, y_like).wait_send()
-    for c in outs:
-        c.wait()
+    for k in (1, 2, 3):
+        y_ring(k, 0).wait_send()
+    y_all.wait_send()
 
 
 def solution(mesh):
@@ -610,7 +647,7 @@
             vm((nd, rows, tg), BF),
             vm((nt - 1, nd, rows // nt, tg), BF),
             vm((nd, rows // nt, tg), BF),
-            vm((rows, tokens), BF),
+            vm((edge, edge, rows // nt, tokens), BF),
             vm((3, mine, tokens), BF),
             vm((nt - 1, 3, mine // edge, tokens // edge), BF),
             vm((3, mine, tokens), BF),
@@ -621,7 +658,6 @@
             vm((group, 2, mine, cols), BF),
             vm((8, LANES), F32),
             vm((group - 1, 8, LANES), F32),
-            vm((rows, cols), F32),
             dma((6,)),
             dma((15,)),
             dma((15,)),
@@ -629,21 +665,26 @@
             dma((12,)),
             dma((4,)),
             dma((4,)),
-            dma((4,)),
-            dma((4,)),
+            dma((3,)),
+            dma((3,)),
             dma((6,)),
             dma((6,)),
+            dma((nd,)),
+            dma((nd,)),
+            dma((2, 2)),
+            dma((2, 2)),
         ]
-        return pl.pallas_call(
+        step = pl.pallas_call(
             functools.partial(kernel, nd, nt, float(width)),
-            out_shape=jax.ShapeDtypeStruct((rows, cols), F32),
+            out_shape=pltpu.VMEM((rows, cols), OT),
             in_specs=[pl.BlockSpec(memory_space=pltpu.HBM)] * 6,
-            out_specs=pl.BlockSpec(memory_space=pltpu.HBM),
+            out_specs=pl.BlockSpec(memory_space=pltpu.VMEM),
             scratch_shapes=scratch,
             compiler_params=pltpu.CompilerParams(
-                collective_id=0, has_side_effects=True, vmem_limit_bytes=67043328
+                collective_id=0, has_side_effects=True, vmem_limit_bytes=60000000
             ),
-        )(embedded, rotation, value_proj, output_proj, mid_exponent, cotangent)
+        )(*[pltpu.with_memory_space_constraint(x, pltpu.HBM) for x in (embedded, rotation, value_proj, output_proj, mid_exponent, cotangent)])
+        return step
 
     return jax.shard_map(
         local,

time: 80.9 us -> 78.3 us (0.968)
  Pallas kernels: 78.9 us -> 77.4 us
  local copies, waits for them, and re-layouts: 1.87 us -> 0.8 us
    pallas_call x1, Pallas kernels: 78.9 us -> 77.4 us  [local(): pl.pallas_call(functools.partial(kernel, nd, nt, float(width)), out_shape...]
    unnamed x1, local copies, waits for them, and re-layouts: 1.87 us -> 0.8 us
where the time goes in v4:
time: 78.3 us; the launch traced here: 78.2 us
  Pallas kernels  77.4 us (99%)
  local copies, waits for them, and re-layouts  0.8 us (1%)
    pallas_call x1, Pallas kernels, local(): pl.pallas_call(functools.partial(kernel, nd, nt, float(width)), out_shape...  77.4 us

profile of v4, /device:TPU:1, one launch (start us, length us, event | category | flops | bytes accessed | tf_op | source)
XLA Modules:
  0.0 78.2 jit_solution(14978537635360330888)
XLA Ops:
  0.0 77.4 %shard_map.64 = f32[512,256]{1,0:T(8,128)S(1)} custom-call(bf16[128,2048]{1,0:T(8,128)(2,1)} %e_hbm.1, f32[512,256]{1,0:T(8,128)} %r_hbm.1, bf16[1,256,1024]{2,1,0:T(8,128)(2,1)} %v_hbm.1, bf16[1,1024,256]{2,1,0:T(8,128)(2,1)} %o_hbm.1, s32[1,1024]{1,0:T(1,128)} %m_hbm.1, bf16[128,256]{1,0:T(8,128)(2,1)} %u_hbm.1), custom_call_target="tpu_custom_call" | custom-call | tf_op jit(solution)/shard_map/pallas_call | solution.py:677
  77.4 0.8 %copy.8 = f32[512,256]{1,0:T(8,128)} copy(f32[512,256]{1,0:T(8,128)S(1)} %shard_map.64) | data formatting | bytes 1048576

commit v5 on v4

--- a/solution.py
+++ b/solution.py
@@ -88,6 +88,7 @@
     yall,
     nsbuf,
     nsrecv,
+    embt,
     insem,
     tsend,
     trecv,
@@ -117,7 +118,7 @@
     tz, ty = t // edge, lax.rem(t, edge)
     tokens = nd * tg
     mine = tg // 2
-    my_side = lax.rem(t, 2)
+    pair = edge // 2
 
     def rcopy(src, dst, ssem, rsem, to):
         return pltpu.make_async_remote_copy(
@@ -146,13 +147,25 @@
             acc = acc + recv[i].astype(F32)
         return acc
 
+    def piece(i, g):
+        return (g // pair) * edge + i * pair + g % pair
+
+    def side(j):
+        return lax.rem(j, edge) // pair
+
+    def unit_group(j):
+        return (j // edge) * pair + lax.rem(lax.rem(j, edge), pair)
+
+    my_side = side(t)
+
     def split(buf, y):
-        for j in range(nt):
-            i, g = j % 2, j // 2
-            buf[j, :own] = y[i * own : (i + 1) * own, g * span : (g + 1) * span].astype(buf.dtype)
+        for i in range(2):
+            for g in range(nt // 2):
+                blk = y[i * own : (i + 1) * own, g * span : (g + 1) * span]
+                buf[piece(i, g), :own] = blk.astype(buf.dtype)
 
     def side_of(buf, i):
-        return jnp.concatenate([buf[2 * g + i, :own] for g in range(nt // 2)], axis=1)
+        return jnp.concatenate([buf[piece(i, g), :own] for g in range(nt // 2)], axis=1)
 
     def join(buf):
         return jnp.concatenate([side_of(buf, 0), side_of(buf, 1)], axis=0)
@@ -198,8 +211,7 @@
             )
         )
     ]
-    for load in loads:
-        load.start()
+    loads[0].start()
 
     bar = pltpu.get_barrier_semaphore()
 
@@ -214,6 +226,8 @@
     greet(partner)
 
     loads[0].wait()
+    for load in loads[1:]:
+        load.start()
     rg[pl.ds(d, 1)] = (r_ref[...] * (1.0 / math.sqrt(width))).astype(BF)[None]
     pl.semaphore_wait(bar, nt - 1 + 2 * (nd - 1) + 1)
 
@@ -266,7 +280,7 @@
         quarter = pbuf.shape[2]
         cross = dot(o_ref[0], v1[:, pl.ds(pl.multiple_of(d * quarter, quarter), quarter)])
         pbuf[...] = cross.astype(BF).reshape(pbuf.shape)
-        to_plane(13, lambda j: pbuf.at[j // 2], lambda i: pbrecv.at[i])
+        to_plane(13, lambda j: pbuf.at[unit_group(j)], lambda i: pbrecv.at[i])
         rs_start(5, e2buf, e2recv)
         d1_copy.wait_recv()
         rs_start(0, dcbuf, dc1recv)
@@ -337,10 +351,10 @@
             for i in range(2):
                 tile = jnp.broadcast_to(to_row(sq[i * own : (i + 1) * own]), (8, LANES))
                 for g in range(nt // 2):
-                    ybuf[2 * g + i, own:] = tile
+                    ybuf[piece(i, g), own:] = tile
 
         def pick(b):
-            g = t // 2
+            g = unit_group(t)
             out = b[0:1, :span]
             for i in range(1, nt // 2):
                 out = jnp.where(g == i, b[0:1, i * span : (i + 1) * span], out)
@@ -361,9 +375,9 @@
             buf[t, own:] = jnp.where(row == 0, hi, jnp.where(row == 1, coef - hi, 0.0)).astype(BF)
 
         def coef_of(buf, i):
-            ext = up(buf[i, own:])
+            ext = up(buf[piece(i, 0), own:])
             for g in range(1, nt // 2):
-                ext = ext + up(buf[2 * g + i, own:])
+                ext = ext + up(buf[piece(i, g), own:])
             return to_col(jnp.sum(ext, axis=0, keepdims=True))
 
         def grad_in(buf, w):
@@ -375,7 +389,7 @@
         rs_start(1, ybuf, y0recv)
         share_inputs()
         plane_wait(13, pbrecv).wait_recv()
-        pall[pl.ds(d, 1)] = total(pbuf[t // 2], pbrecv).astype(BF)[None]
+        pall[pl.ds(d, 1)] = total(pbuf[unit_group(t)], pbrecv).astype(BF)[None]
         to_ring(3, lambda j: pall.at[d], lambda j: pall.at[d])
         tot0 = rs_total(1, ybuf, y0recv)
         inv0 = norm(tot0)
@@ -395,11 +409,22 @@
         rs_start(14, hobuf, horecv)
         tot1 = rs_total(3, ybuf, y1recv)
         gate(tot1, dc1, norm(tot1), bound1, qbuf)
-        ag_start(4, qbuf)
+        mates, rest = [], []
+        for a in (2, 1, 3, 0):
+            row = lax.rem(tz + a, edge) * edge
+            for c in range(pair - 1, -1, -1):
+                if a or c:
+                    mates.append(row + my_side * pair + lax.rem(ty + c, pair))
+                rest.append(row + (1 - my_side) * pair + lax.rem(ty + c, pair))
+        for ph, targets in ((4, mates), (15, rest)):
+            for j in targets:
+                rcopy(qbuf.at[t], qbuf.at[t], tsend.at[ph], trecv.at[ph], (p, d, j)).start()
+        q_mates = plane_wait(4, qbuf.at[pl.ds(0, nt // 2 - 1)])
+        q_rest = plane_wait(15, qbuf.at[pl.ds(0, nt // 2)])
         ho = rs_total(14, hobuf, horecv)
         p_three = pall.at[pl.ds(0, nd - 1)]
         ring_wait(3, p_three).wait_recv()
-        ag_wait(4, qbuf)
+        q_mates.wait_recv()
         q1 = side_of(qbuf, my_side)
         quarter = pall.shape[2]
         dc0 = e2 - coef_of(qbuf, my_side) * ho
@@ -407,6 +432,7 @@
             dc0 = dc0 + dot_nt(q1[:, i * quarter : (i + 1) * quarter], pall[i])
         gate(tot0, dc0, inv0, bound0, q0buf)
         ag_start(6, q0buf)
+        q_rest.wait_recv()
         lin, coef = grad_in(qbuf, v1[...])
         u1 = (up(u_ref[...]) + lin - coef * up(h1)).astype(BF)
         ag_wait(6, q0buf)
@@ -421,7 +447,9 @@
     def _():
         share_inputs()
         ring_wait(0, xall.at[pl.ds(0, nd - 1)]).wait_recv()
-        xgram[0] = dot_nt(xall[d], xall[...].reshape(tokens, xall.shape[2])).astype(BF)
+        pair = pl.ds(pl.multiple_of(lax.rem(d, 2) * mine, mine), mine)
+        both = jnp.concatenate([xall[i * (nd // 2) + d // 2, pair] for i in range(2)], axis=0)
+        xgram[0] = dot_nt(both, xall[...].reshape(tokens, xall.shape[2])).astype(BF)
         gram_start(10, xgram, xgramrecv)
         gram_turn(10, xgram, xgramrecv, xgramall)
         plane_wait(11, xgramrecv).wait_recv()
@@ -438,7 +466,8 @@
 
     to_plane(7, lambda j: vpart.at[:, vspot(j)], lambda i: vrecv.at[i])
 
-    my_rows = pl.ds(pl.multiple_of(p * mine, mine), mine)
+    my_group = p * (nd // 2) + d // 2
+    my_rows = pl.ds(pl.multiple_of(lax.rem(d, 2) * mine, mine), mine)
     g_three = gall.at[pl.ds(0, nd - 1)]
 
     @pl.when(p == 0)
@@ -451,8 +480,8 @@
         rcopy(g_three, g_three, gsend.at[1], grecv.at[1], partner).wait_recv()
 
     hid = xall[...].reshape(tokens, xall.shape[2])
-    g_mine = gall[d, my_rows]
-    x_mine = xall[d, my_rows]
+    g_mine = gall[my_group, my_rows]
+    x_mine = xall[my_group, my_rows]
     grad = gall[...].reshape(tokens, gall.shape[2])
     gram[0] = dot_nt(g_mine, hid).astype(BF)
     gram[1] = dot_nt(g_mine, grad).astype(BF)
@@ -491,7 +520,7 @@
 
     e_three = eall.at[pl.ds(0, nd - 1)]
     ring_wait(1, e_three).wait_recv()
-    emb_t = eall[...].reshape(tokens, rows).T
+    embt[...] = eall[...].reshape(tokens, rows).T
 
     @pl.when(p == 0)
     def _():
@@ -513,10 +542,10 @@
 
     nsbuf[...] = jnp.broadcast_to(8.0 * jnp.sum(up(x_x) * up(g_g) - up(g_x) * up(x_g)), nsbuf.shape)
     to_group(2, nsbuf, lambda k: nsrecv.at[k - 1])
-    place = d * 2 + p
+    place = slot
 
     def y_ring(k, to):
-        blk = yall.at[lax.rem(d + to, nd) * 2 + p]
+        blk = yall.at[p * nd + lax.rem(d + to, nd)]
         return rcopy(blk, blk, ysend.at[k], yrecv.at[k], (p, ring(k), t))
 
     def y_chip(i):
@@ -531,7 +560,10 @@
 
     for c in v_waits(1):
         c.wait_recv()
-    vt = vall[...].reshape(rows, tokens)
+
+    def vt_of(lanes):
+        return vall[:, :, :, lanes].reshape(rows, tokens // 2)
+
     group_wait(2, nsrecv).wait_recv()
     ns = nsbuf[...]
     for k in range(group - 1):
@@ -540,18 +572,23 @@
     scale = math.sqrt(width)
     for k in (1, 3, 2):
         y_ring(k, nd - k).wait_recv()
-        y_chip(lax.rem(d + nd - k, nd) * 2 + p).start()
+        y_chip(p * nd + lax.rem(d + nd - k, nd)).start()
     y_like = yall.at[pl.ds(0, nd)]
     y_all = rcopy(y_like, y_like, ysend.at[0], yrecv.at[0], partner)
+
+    cut = tokens // 2
+
+    def part_of(i):
+        pieces = yall[pl.ds(i * nd, nd)]
+        groups = pl.ds(i * (nd // 2), nd // 2)
+        za = 2.0 * up(gall[groups].reshape(cut, -1)) - 0.5 * rate * up(pieces[:, 0].reshape(cut, -1))
+        zb = -2.0 * up(xall[groups].reshape(cut, -1)) - 0.5 * rate * up(pieces[:, 1].reshape(cut, -1))
+        lanes = pl.ds(pl.multiple_of(i * cut, cut), cut)
+        return dot(embt[:, lanes], za.astype(BF)) + dot(vt_of(lanes), zb.astype(BF))
+
+    out_ref[...] = r_ref[...] - (0.5 * scale) * rate * part_of(p)
     y_all.wait_recv()
-    half_rate = -0.5 * rate
-    za = (2.0 * up(grad) + half_rate * up(yall[:, 0].reshape(tokens, -1))).astype(BF)
-    zb = (-2.0 * up(hid) + half_rate * up(yall[:, 1].reshape(tokens, -1))).astype(BF)
-    cut = rows // 4
-    for i in range(4):
-        blk = slice(i * cut, (i + 1) * cut)
-        last = dot(emb_t[blk], za) + dot(vt[blk], zb)
-        out_ref[blk] = r_ref[blk] - (0.5 * scale) * rate * last
+    out_ref[...] = out_ref[...] - (0.5 * scale) * rate * part_of(1 - p)
 
     for c in r_sends + r_on:
         c.wait_send()
@@ -565,7 +602,8 @@
         plane_wait(0, like(dcbuf)).wait_send()
         plane_wait(2, like(cbuf)).wait_send()
         plane_wait(3, like(ybuf)).wait_send()
-        plane_wait(4, like(qbuf)).wait_send()
+        plane_wait(4, qbuf.at[pl.ds(0, nt // 2 - 1)]).wait_send()
+        plane_wait(15, qbuf.at[pl.ds(0, nt // 2)]).wait_send()
         plane_wait(5, like(e2buf)).wait_send()
         plane_wait(6, like(q0buf)).wait_send()
         plane_wait(13, pbrecv).wait_send()
@@ -658,9 +696,10 @@
             vm((group, 2, mine, cols), BF),
             vm((8, LANES), F32),
             vm((group - 1, 8, LANES), F32),
+            vm((rows, tokens), BF),
             dma((6,)),
-            dma((15,)),
-            dma((15,)),
+            dma((16,)),
+            dma((16,)),
             dma((12,)),
             dma((12,)),
             dma((4,)),

time: 78.3 us -> 77.1 us (0.985)
  Pallas kernels: 77.4 us -> 76.1 us
    pallas_call x1, Pallas kernels: 77.4 us -> 76.1 us  [local(): pl.pallas_call(functools.partial(kernel, nd, nt, float(width)), out_shape...]
where the time goes in v5:
time: 77.1 us; the launch traced here: 76.9 us
  Pallas kernels  76.1 us (99%)
  local copies, waits for them, and re-layouts  0.8 us (1%)
    pallas_call x1, Pallas kernels, local(): pl.pallas_call(functools.partial(kernel, nd, nt, float(width)), out_shape...  76.1 us

profile of v5, /device:TPU:1, one launch (start us, length us, event | category | flops | bytes accessed | tf_op | source)
XLA Modules:
  0.0 76.9 jit_solution(17248281183396696237)
XLA Ops:
  0.0 76.1 %shard_map.64 = f32[512,256]{1,0:T(8,128)S(1)} custom-call(bf16[128,2048]{1,0:T(8,128)(2,1)} %e_hbm.1, f32[512,256]{1,0:T(8,128)} %r_hbm.1, bf16[1,256,1024]{2,1,0:T(8,128)(2,1)} %v_hbm.1, bf16[1,1024,256]{2,1,0:T(8,128)(2,1)} %o_hbm.1, s32[1,1024]{1,0:T(1,128)} %m_hbm.1, bf16[128,256]{1,0:T(8,128)(2,1)} %u_hbm.1), custom_call_target="tpu_custom_call" | custom-call | tf_op jit(solution)/shard_map/pallas_call | solution.py:716
  76.1 0.8 %copy.8 = f32[512,256]{1,0:T(8,128)} copy(f32[512,256]{1,0:T(8,128)S(1)} %shard_map.64) | data formatting | bytes 1048576

commit v6 on v5

--- a/solution.py
+++ b/solution.py
@@ -30,7 +30,8 @@
 
 def far_first(edge):
     cells = [(a, b) for a in range(edge) for b in range(edge) if a or b]
-    return sorted(cells, key=lambda c: -min(c[0], edge - c[0]) - min(c[1], edge - c[1]))
+    hops = [[min(x, edge - x) for x in c] for c in cells]
+    return [c for _, c in sorted(zip(hops, cells), key=lambda h: (-sum(h[0]), -h[0][0] if sum(h[0]) > 1 else h[0][0]))]
 
 
 def kernel(
@@ -558,8 +559,6 @@
         y_ring(k, 0).start()
     y_chip(place).start()
 
-    for c in v_waits(1):
-        c.wait_recv()
 
     def vt_of(lanes):
         return vall[:, :, :, lanes].reshape(rows, tokens // 2)
@@ -573,6 +572,8 @@
     for k in (1, 3, 2):
         y_ring(k, nd - k).wait_recv()
         y_chip(p * nd + lax.rem(d + nd - k, nd)).start()
+    for c in v_waits(1):
+        c.wait_recv()
     y_like = yall.at[pl.ds(0, nd)]
     y_all = rcopy(y_like, y_like, ysend.at[0], yrecv.at[0], partner)
 

time: 77.1 us -> 76.5 us (level)
  no operation moved by 1% of the time
where the time goes in v6:
time: 76.5 us; the launch traced here: 76.4 us
  Pallas kernels  75.6 us (99%)
  local copies, waits for them, and re-layouts  0.8 us (1%)
    pallas_call x1, Pallas kernels, local(): pl.pallas_call(functools.partial(kernel, nd, nt, float(width)), out_shape...  75.6 us

profile of v6, /device:TPU:1, one launch (start us, length us, event | category | flops | bytes accessed | tf_op | source)
XLA Modules:
  0.0 76.4 jit_solution(8443402050509583061)
XLA Ops:
  0.0 75.6 %shard_map.64 = f32[512,256]{1,0:T(8,128)S(1)} custom-call(bf16[128,2048]{1,0:T(8,128)(2,1)} %e_hbm.1, f32[512,256]{1,0:T(8,128)} %r_hbm.1, bf16[1,256,1024]{2,1,0:T(8,128)(2,1)} %v_hbm.1, bf16[1,1024,256]{2,1,0:T(8,128)(2,1)} %o_hbm.1, s32[1,1024]{1,0:T(1,128)} %m_hbm.1, bf16[128,256]{1,0:T(8,128)(2,1)} %u_hbm.1), custom_call_target="tpu_custom_call" | custom-call | tf_op jit(solution)/shard_map/pallas_call | solution.py:717
  75.6 0.8 %copy.8 = f32[512,256]{1,0:T(8,128)} copy(f32[512,256]{1,0:T(8,128)S(1)} %shard_map.64) | data formatting | bytes 1048576

commit v7 on v6

--- a/solution.py
+++ b/solution.py
@@ -82,10 +82,8 @@
     gram,
     gramrecv,
     gramall,
-    xgram,
-    xgramrecv,
-    xgramall,
-    xx,
+    eebuf,
+    eerecv,
     yall,
     nsbuf,
     nsrecv,
@@ -262,7 +260,6 @@
     b1_copy = rcopy(bnd, bnd1, psend.at[1], precv.at[1], partner)
     d1_copy = rcopy(dcbuf, dcbuf, psend.at[2], precv.at[2], partner)
     x_copy = rcopy(xpart, xrecv, psend.at[3], precv.at[3], partner)
-    xx_copy = rcopy(xgramall.at[0, pl.ds(0, mine)], xx, psend.at[4], precv.at[4], partner)
     g_copy = rcopy(gall.at[d], gall.at[d], psend.at[5], precv.at[5], partner)
 
     bnd[...] = jnp.broadcast_to(jnp.exp2(m_ref[...].astype(F32)), bnd.shape)
@@ -304,6 +301,22 @@
     x_copy.start()
     x_copy.wait_recv()
     xall[pl.ds(d, 1)] = (up(xpart[...]) + up(xrecv[...])).astype(BF)[None]
+
+    def to_group(ph, src, dst):
+        for k in (6, 2, 5, 7, 1, 3, 4):
+            j = lax.rem(slot + k, group)
+            rcopy(src(j), dst(k), gsend.at[ph], grecv.at[ph], (j // nd, lax.rem(j, nd), t)).start()
+
+    def group_wait(ph, like):
+        return rcopy(like, like, gsend.at[ph], grecv.at[ph], partner)
+
+    e_three = eall.at[pl.ds(0, nd - 1)]
+
+    def share_gram():
+        ring_wait(1, e_three).wait_recv()
+        emb = eall[...].reshape(tokens, rows)
+        eebuf[...] = dot_nt(emb, emb).astype(BF).reshape(eebuf.shape)
+        to_group(3, lambda j: eebuf.at[j], lambda k: eerecv.at[k - 1])
 
     def share_inputs():
         to_ring(0, lambda j: xall.at[d], lambda j: xall.at[d])
@@ -422,6 +435,7 @@
                 rcopy(qbuf.at[t], qbuf.at[t], tsend.at[ph], trecv.at[ph], (p, d, j)).start()
         q_mates = plane_wait(4, qbuf.at[pl.ds(0, nt // 2 - 1)])
         q_rest = plane_wait(15, qbuf.at[pl.ds(0, nt // 2)])
+        share_gram()
         ho = rs_total(14, hobuf, horecv)
         p_three = pall.at[pl.ds(0, nd - 1)]
         ring_wait(3, p_three).wait_recv()
@@ -447,15 +461,8 @@
     @pl.when(p == 1)
     def _():
         share_inputs()
+        share_gram()
         ring_wait(0, xall.at[pl.ds(0, nd - 1)]).wait_recv()
-        pair = pl.ds(pl.multiple_of(lax.rem(d, 2) * mine, mine), mine)
-        both = jnp.concatenate([xall[i * (nd // 2) + d // 2, pair] for i in range(2)], axis=0)
-        xgram[0] = dot_nt(both, xall[...].reshape(tokens, xall.shape[2])).astype(BF)
-        gram_start(10, xgram, xgramrecv)
-        gram_turn(10, xgram, xgramrecv, xgramall)
-        plane_wait(11, xgramrecv).wait_recv()
-        xx[...] = xgramall[0, pl.ds(mine, mine)]
-        xx_copy.start()
         g_copy.wait_recv()
 
     vsum = dot_nt(rg[...].reshape(nd * rows, rg.shape[2]), gall[d]).astype(BF)
@@ -519,30 +526,22 @@
     ring_wait(2, v_three).wait_recv()
     v_turn(0)
 
-    e_three = eall.at[pl.ds(0, nd - 1)]
-    ring_wait(1, e_three).wait_recv()
     embt[...] = eall[...].reshape(tokens, rows).T
 
-    @pl.when(p == 0)
-    def _():
-        xx_copy.wait_recv()
+    group_wait(3, eerecv).wait_recv()
+    ee = up(eebuf[slot])
+    for k in range(group - 1):
+        ee = ee + up(eerecv[k])
+    x_x = ee.astype(BF)
 
     for c in v_waits(0):
         c.wait_recv()
     v_turn(1)
     plane_wait(9, gramrecv).wait_recv()
-    g_x, g_g, x_g, x_x = gramall[0], gramall[1], gramall[2], xx[...]
-
-    def to_group(ph, src, dst):
-        for k in (6, 2, 5, 7, 1, 3, 4):
-            j = lax.rem(slot + k, group)
-            rcopy(src, dst(k), gsend.at[ph], grecv.at[ph], (j // nd, lax.rem(j, nd), t)).start()
-
-    def group_wait(ph, like):
-        return rcopy(like, like, gsend.at[ph], grecv.at[ph], partner)
+    g_x, g_g, x_g = gramall[0], gramall[1], gramall[2]
 
     nsbuf[...] = jnp.broadcast_to(8.0 * jnp.sum(up(x_x) * up(g_g) - up(g_x) * up(x_g)), nsbuf.shape)
-    to_group(2, nsbuf, lambda k: nsrecv.at[k - 1])
+    to_group(2, lambda j: nsbuf, lambda k: nsrecv.at[k - 1])
     place = slot
 
     def y_ring(k, to):
@@ -619,9 +618,6 @@
         d1_copy.wait_send()
         b1_copy.wait_send()
         v1_copy.wait_send()
-        plane_wait(10, xgramrecv).wait_send()
-        plane_wait(11, xgramrecv).wait_send()
-        xx_copy.wait_send()
 
     plane_wait(7, vrecv).wait_send()
     plane_wait(8, gramrecv).wait_send()
@@ -630,6 +626,7 @@
         for c in v_waits(step):
             c.wait_send()
     group_wait(2, nsrecv).wait_send()
+    group_wait(3, eerecv).wait_send()
     for k in (1, 2, 3):
         y_ring(k, 0).wait_send()
     y_all.wait_send()
@@ -690,10 +687,8 @@
             vm((3, mine, tokens), BF),
             vm((nt - 1, 3, mine // edge, tokens // edge), BF),
             vm((3, mine, tokens), BF),
-            vm((1, tg, tokens), BF),
-            vm((nt - 1, 1, tg // edge, tokens // edge), BF),
-            vm((1, tg, tokens), BF),
-            vm((mine, tokens), BF),
+            vm((group, mine, tokens), BF),
+            vm((group - 1, mine, tokens), BF),
             vm((group, 2, mine, cols), BF),
             vm((8, LANES), F32),
             vm((group - 1, 8, LANES), F32),
@@ -705,8 +700,8 @@
             dma((12,)),
             dma((4,)),
             dma((4,)),
-            dma((3,)),
-            dma((3,)),
+            dma((4,)),
+            dma((4,)),
             dma((6,)),
             dma((6,)),
             dma((nd,)),

time: 76.5 us -> 76.1 us (level)
  no operation moved by 1% of the time
where the time goes in v7:
time: 76.1 us; the launch traced here: 76 us
  Pallas kernels  75.2 us (99%)
  local copies, waits for them, and re-layouts  0.8 us (1%)
    pallas_call x1, Pallas kernels, local(): pl.pallas_call(functools.partial(kernel, nd, nt, float(width)), out_shape...  75.2 us

profile of v7, /device:TPU:1, one launch (start us, length us, event | category | flops | bytes accessed | tf_op | source)
XLA Modules:
  0.0 76.0 jit_solution(119437850709119312)
XLA Ops:
  0.0 75.2 %shard_map.64 = f32[512,256]{1,0:T(8,128)S(1)} custom-call(bf16[128,2048]{1,0:T(8,128)(2,1)} %e_hbm.1, f32[512,256]{1,0:T(8,128)} %r_hbm.1, bf16[1,256,1024]{2,1,0:T(8,128)(2,1)} %v_hbm.1, bf16[1,1024,256]{2,1,0:T(8,128)(2,1)} %o_hbm.1, s32[1,1024]{1,0:T(1,128)} %m_hbm.1, bf16[128,256]{1,0:T(8,128)(2,1)} %u_hbm.1), custom_call_target="tpu_custom_call" | custom-call | tf_op jit(solution)/shard_map/pallas_call | solution.py:712
  75.2 0.8 %copy.8 = f32[512,256]{1,0:T(8,128)} copy(f32[512,256]{1,0:T(8,128)S(1)} %shard_map.64) | data formatting | bytes 1048576
